TPU v7x, 128 devices: a whole 4x4x4 slice. The times are simulated.
128 devices in a mesh: dp: 2 (over y_lo), ctx: 64 (over x, y_hi, z, core).
Axes of the slice: x: 4, y: 4 (y_hi: 2, y_lo: 2; y = y_hi * 2 + y_lo), z: 4, core: 2. Of those that a mesh axis runs over, the one named last changes fastest.
Arguments:
- tokens: bfloat16 [2, 24576, 2560], P('dp', 'ctx'), may hold values from -32 to 32
- qkv_weight: bfloat16 [2560, 3840], P(None, 'dp'), may hold values from -8 to 8
- out_weight: bfloat16 [1280, 2560], P(None, 'dp'), may hold values from -3.5 to 3.5
- offsets: int32 [4, 10], replicated, may hold values from 0 to 7, as said below
Outputs:
- mixed: bfloat16 [2, 24576, 2560], P('dp', 'ctx')
Inputs may be any that keep to these rules, and one draw needn't show every extreme that they name: offsets[j, h] is at most 2 ** j - 1 for level j.
All inputs are finite; a program needn't handle non-finite values.
Results may differ from a plain program's by a relative error of at most 0.0083.
Values may be sent and summed in bfloat16 or wider, within the bound.
No kernel may reach another device: no remote copies, remote signals or barrier semaphores. Data moves between devices by JAX's collectives and lax.ppermute only.
A program may use at most 192 MiB of HBM per device.

v0:
```python
import jax
import jax.numpy as jnp
from jax import lax
from jax.experimental import pallas as pl
from jax.experimental.pallas import tpu as pltpu
from jax.sharding import PartitionSpec as P


TOK = 384
ROWS = 2 * TOK
HD = 128
HH = 5
WB = HH * HD
LEVELS = 4
KC = 1280
LOG2E = 1.4426950408889634

META_CORE, META_FSRC, _, META_SSRC, _, META_QSRC, _, META_FK, META_DP = range(9)
META_OFF = 16


def lin(x, y, z, c):
    return (y % 2) * 64 + (((x % 4) * 2 + (y % 4) // 2) * 4 + z % 4) * 2 + c


def send(block, target):
    route = []
    for x in range(4):
        for y in range(4):
            for z in range(4):
                for c in range(2):
                    goal = target(x, y, z, c)
                    if goal is not None:
                        route.append((lin(x, y, z, c), lin(*goal)))
    return lax.ppermute(block, ("dp", "ctx"), route)


def to_core(x, y, z, c):
    return (x, y, z, 1 - c)


def to_y(x, y, z, c):
    return (x, y - 1 if c == 0 else y + 1, z, c)


def to_x(x, y, z, c):
    return (x - 1 if c == 0 else x + 1, y, z, c)


def to_z1(x, y, z, c):
    return (x, y, z ^ 1, c)


def to_z3(x, y, z, c):
    return (x, y, z ^ 3, c)


def to_y2(x, y, z, c):
    return (x, y + 2, z, c)


def held(*arrays):
    return [pltpu.with_memory_space_constraint(a, pltpu.VMEM) for a in arrays]


def far(*arrays):
    return [pltpu.with_memory_space_constraint(a, pltpu.HBM) for a in arrays]


HELD = pl.BlockSpec(memory_space=pltpu.VMEM)
SCALARS = pl.BlockSpec(memory_space=pltpu.SMEM)
FAR = pl.BlockSpec(memory_space=pltpu.HBM)


def params(mib):
    return pltpu.CompilerParams(vmem_limit_bytes=mib << 20)


def stage_kernel(x_own, x_oth, x_all, sem):
    copies = [pltpu.make_async_copy(x, x_all.at[pl.ds(g * TOK, TOK)], sem.at[g]) for g, x in enumerate((x_own, x_oth))]
    for copy in copies:
        copy.start()
    for copy in copies:
        copy.wait()


def stage(x_own, x_oth):
    return pl.pallas_call(
        stage_kernel,
        out_shape=pltpu.VMEM((ROWS, x_own.shape[1]), x_own.dtype),
        in_specs=[FAR, FAR],
        out_specs=HELD,
        scratch_shapes=[pltpu.SemaphoreType.DMA((2,))],
        compiler_params=params(6),
        name="stage",
    )(*far(x_own, x_oth))


def payload_kernel(block, w, out, sem):
    core = lax.axis_index("ctx") % 2
    half = w.shape[0] // 2
    rows = pl.ds(pl.multiple_of(core * half, half), half)
    copy = pltpu.make_async_copy(w.at[rows, pl.ds(pl.multiple_of(block() * WB, HD), WB)], out, sem.at[0])
    copy.start()
    copy.wait()


def payload(block, w):
    return pl.pallas_call(
        lambda *refs: payload_kernel(block, *refs),
        out_shape=pltpu.VMEM((w.shape[0] // 2, WB), w.dtype),
        in_specs=[FAR],
        out_specs=HELD,
        scratch_shapes=[pltpu.SemaphoreType.DMA((1,))],
        compiler_params=params(6),
    )(*far(w))


def first_block():
    odd = (lax.axis_index("ctx") // 16) % 2
    return 2 - 2 * lax.rem(lax.axis_index("dp") + odd, 2)


CUT2, CUT3 = ROWS >> 2, (ROWS >> 2) + (ROWS >> 3)


def proj_kernel(remote, slot, for_keys, meta, x_all, w_loc, *rest):
    halves = rest[: 2 * remote]
    outs, (wbuf, acc, wsem) = rest[2 * remote : -3], rest[-3:]
    chunks = w_loc.shape[0] // KC
    core = meta[META_CORE]
    src = meta[slot]
    col = pl.multiple_of(meta[slot + 1] * WB, HD)
    for i in range(chunks):
        rows = pl.ds(i * KC, KC)

        @pl.when(src == 0)
        def _():
            pltpu.make_async_copy(w_loc.at[rows, pl.ds(col, WB)], wbuf.at[rows], wsem.at[i]).start()

        part = i * 2 // chunks
        low = pl.ds((i - part * (chunks // 2)) * KC, KC)
        for r in range(remote):
            for own in range(2):

                @pl.when((src == r + 1) & ((core == part) if own else (core != part)))
                def _():
                    pltpu.make_async_copy(halves[2 * r + 1 - own].at[low], wbuf.at[rows], wsem.at[i]).start()

    for i in range(chunks):
        rows = pl.ds(i * KC, KC)
        pltpu.make_async_copy(w_loc.at[rows, pl.ds(0, WB)], wbuf.at[rows], wsem.at[i]).wait()
        for g in range(2):
            span = pl.ds(g * TOK, TOK)
            got = jnp.dot(x_all[span, rows], wbuf[rows], preferred_element_type=jnp.float32)
            for h in range(HH):
                piece = got[:, h * HD : (h + 1) * HD]
                if i > 0:
                    piece = acc[h, span] + piece
                acc[h, span] = piece
                if i == chunks - 1:
                    outs[0][span, pl.ds(h * HD, HD)] = piece.astype(jnp.bfloat16)
    for h in range(HH):
        cols = pl.ds(h * HD, HD)
        kept = [
            acc[h, pl.ds(meta[META_OFF + j * HH + h], ROWS >> j, stride=1 << j), :].astype(jnp.bfloat16)
            for j in range(1, LEVELS)
        ]
        outs[1][:, cols] = kept[0]
        outs[2][pl.ds(0, CUT2), cols] = kept[1]
        outs[2][pl.ds(CUT2, ROWS >> 3), cols] = kept[2]
        if for_keys:
            outs[2][pl.ds(CUT3, ROWS >> 3), cols] = kept[2]
            outs[3][:, cols] = kept[2]


def project(meta, slot, x_all, w_loc, remotes, for_keys):
    depth = w_loc.shape[0]
    flat = [half for pair in remotes for half in pair]
    shapes = [(ROWS, WB), (ROWS >> 1, WB)] + ([(ROWS >> 1, WB), (ROWS >> 3, WB)] if for_keys else [(CUT3, WB)])
    return pl.pallas_call(
        lambda *refs: proj_kernel(len(remotes), slot, for_keys, *refs),
        out_shape=[pltpu.VMEM(s, jnp.bfloat16) for s in shapes],
        in_specs=[SCALARS, HELD] + [FAR] * (1 + len(flat)),
        out_specs=[HELD] * len(shapes),
        scratch_shapes=[
            pltpu.VMEM((depth, WB), jnp.bfloat16),
            pltpu.VMEM((HH, ROWS, HD), jnp.float32),
            pltpu.SemaphoreType.DMA((depth // KC,)),
        ],
        compiler_params=params(16),
        cost_estimate=pl.CostEstimate(
            flops=2 * ROWS * depth * WB, transcendentals=0, bytes_accessed=2 * (ROWS * depth + depth * WB + 2 * ROWS * WB)
        ),
    )(meta, *held(x_all), *far(w_loc, *flat))


def softmax_rows(q, keys, values, factor):
    scores = [lax.dot_general(q, k, (((1,), (1,)), ((), ())), preferred_element_type=jnp.float32) for k in keys]
    top = scores[0].max(axis=1, keepdims=True)
    for s in scores[1:]:
        top = jnp.maximum(top, s.max(axis=1, keepdims=True))
    total, blend = 0.0, 0.0
    for s, v in zip(scores, values):
        e = jnp.exp2((s - top) * factor)
        total = total + e.sum(axis=1, keepdims=True)
        blend = blend + jnp.dot(e.astype(jnp.bfloat16), v, preferred_element_type=jnp.float32)
    return blend, top * factor, total


def pack(top, total):
    lane = lax.broadcasted_iota(jnp.int32, (1, HD), 1)
    return jnp.where(lane == 0, top, total)


def merge(acc_ref, ml_ref, where, blend, top, total):
    old = ml_ref[where]
    old_top, old_total = old[:, 0:1], old[:, 1:2]
    newest = jnp.maximum(old_top, top)
    former, fresh = jnp.exp2(old_top - newest), jnp.exp2(top - newest)
    acc_ref[where] = acc_ref[where] * former + blend * fresh
    ml_ref[where] = pack(newest, old_total * former + total * fresh)


def choose(meta, firsts, seconds, cut, cols):
    f_is_k = jnp.full((1, 1), meta[META_FK], jnp.int32) == 1
    keys, values = [], []
    for f_ref, s_ref in zip(firsts, seconds):
        f, s = f_ref[cut, cols], s_ref[cut, cols]
        keys.append(jnp.where(f_is_k, f, s))
        values.append(jnp.where(f_is_k, s, f))
    return keys, values


def level0_kernel(factor, meta, q_ref, f_ref, s_ref, acc_ref, ml_ref):
    for h in range(HH):
        cols = pl.ds(h * HD, HD)
        keys, values = choose(meta, [f_ref], [s_ref], slice(None), cols)
        for start in range(0, ROWS, TOK):
            blend, top, total = softmax_rows(q_ref[pl.ds(start, TOK), cols], keys, values, factor)
            acc_ref[h, pl.ds(start, TOK), :] = blend
            ml_ref[h, pl.ds(start, TOK), :] = pack(top, total)


def level1_kernel(factor, meta, q_ref, f0, f1, s0, s1, _acc, _ml, acc_ref, ml_ref):
    for h in range(HH):
        cols = pl.ds(h * HD, HD)
        keys, values = choose(meta, [f0, f1], [s0, s1], slice(None), cols)
        where = (h, pl.ds(meta[META_OFF + HH + h], TOK, stride=2), slice(None))
        merge(acc_ref, ml_ref, where, *softmax_rows(q_ref[:, cols], keys, values, factor))


def level23_kernel(factor, meta, q_ref, f0, f1, f2, f3, s0, s1, s2, s3, _acc, _ml, own_ref, oth_ref, acc, ml):
    for h in range(HH):
        cols = pl.ds(h * HD, HD)
        for level, low, rows in ((2, 0, CUT2), (3, CUT2, ROWS >> 3)):
            cut = slice(0, CUT2) if level == 2 else slice(CUT2, ROWS >> 1)
            keys, values = choose(meta, [f0, f1, f2, f3], [s0, s1, s2, s3], cut, cols)
            where = (h, pl.ds(meta[META_OFF + level * HH + h], rows, stride=1 << level), slice(None))
            merge(acc, ml, where, *softmax_rows(q_ref[pl.ds(low, rows), cols], keys, values, factor))
        share = acc[h] * (1.0 / ml[h][:, 1:2])
        own_ref[:, cols] = share[:TOK].astype(jnp.bfloat16)
        oth_ref[:, cols] = share[TOK:].astype(jnp.bfloat16)


STATE = [((HH, ROWS, HD), jnp.float32)] * 2


def attend(kernel, meta, arrays, outs, rows, alias=None):
    factor = HD ** (-0.5) * LOG2E
    return pl.pallas_call(
        lambda *refs: kernel(factor, *refs),
        out_shape=[pltpu.VMEM(*o) for o in outs],
        in_specs=[SCALARS] + [HELD] * len(arrays),
        out_specs=[HELD] * len(outs),
        input_output_aliases=alias or {},
        compiler_params=params(20),
        cost_estimate=pl.CostEstimate(
            flops=4 * rows * ROWS * WB, transcendentals=rows * ROWS * HH, bytes_accessed=2 * (rows + 2 * ROWS) * WB
        ),
    )(meta, *held(*arrays))


def tile_of(t, core_rows, w_loc, rem):
    cols = pl.ds((t % 2) * WB, WB)
    return w_loc[core_rows, cols] if t < 2 else rem[:, cols]


def out_own_kernel(meta, att, w_loc, rem, part):
    rows = pl.ds(pl.multiple_of(meta[META_CORE] * WB, HD), WB)
    for t in range(4):
        part[t] = jnp.dot(att[...], tile_of(t, rows, w_loc, rem), preferred_element_type=jnp.float32)


def out_oth_kernel(meta, att, w_loc, rem, part, out, buf, sem):
    rows = pl.ds(pl.multiple_of((1 - meta[META_CORE]) * WB, HD), WB)
    d = meta[META_DP]
    copies = []
    for t in range(4):
        got = part[t] + jnp.dot(att[...], tile_of(t, rows, w_loc, rem), preferred_element_type=jnp.float32)
        buf[t] = got.astype(jnp.bfloat16)
        col = (d if t < 2 else 1 - d) * (2 * WB) + (t % 2) * WB
        copies.append(pltpu.make_async_copy(buf.at[t], out.at[:, pl.ds(pl.multiple_of(col, HD), WB)], sem.at[t]))
        copies[-1].start()
    for copy in copies:
        copy.wait()


def out_project(kernel, meta, arrays, out_shape, out_spec, scratch):
    return pl.pallas_call(
        kernel,
        out_shape=out_shape,
        in_specs=[SCALARS] + [HELD] * len(arrays),
        out_specs=out_spec,
        scratch_shapes=scratch,
        compiler_params=params(16),
        cost_estimate=pl.CostEstimate(flops=8 * TOK * WB * WB, transcendentals=0, bytes_accessed=8 * WB * WB + 8 * TOK * WB),
    )(meta, *held(*arrays))


def local(tokens, qkv_weight, out_weight, offsets):
    d = lax.axis_index("dp")
    ctx = lax.axis_index("ctx")
    core = ctx & 1
    odd = (ctx >> 4) & 1
    depth = qkv_weight.shape[0]

    pick = lambda a0, a1, b0, b1: jnp.where(d == 0, jnp.where(core == 0, a0, a1), jnp.where(core == 0, b0, b1))
    f_src, f_blk = pick(0, 1, 0, 0), pick(2, 0, 1, 0)
    s_src, s_blk = pick(3, 2, 1 + odd, 0), pick(0, 0, 0, 2)
    q_src, q_blk = pick(0, 0, 2 - odd, 3), pick(0, 1, 0, 0)
    f_is_k = pick(1, 1 - odd, 0, 1)
    zero = jnp.zeros((), jnp.int32)
    heads = lax.dynamic_slice(offsets, (0, core * HH), (LEVELS, HH)).reshape(-1)
    meta = jnp.concatenate(
        [jnp.stack([core, f_src, f_blk, s_src, s_blk, q_src, q_blk, f_is_k, d] + [zero] * 7).astype(jnp.int32), heads]
    )

    x_own = tokens.reshape(TOK, depth)
    first_own = send(payload(first_block, qkv_weight), to_y)
    x_oth = send(x_own, to_core)
    side_own = send(payload(lambda: 1, qkv_weight), to_y)
    x_all = stage(x_own, x_oth)
    first_fwd = send(first_own, to_core)
    relay_own = send(first_own, to_x)
    relay_fwd = send(relay_own, to_core)
    side_fwd = send(side_own, to_core)

    def gather(block):
        far = send(block[3], to_y2)
        joined = lax.dynamic_update_slice(block[2], far, (CUT3, 0))
        pair = send(joined, to_z1)
        ring = send(joined, to_z3)
        relay = send(pair, to_z3)
        return (joined, pair, ring, relay), send(block[1], to_z1)

    first = project(meta, META_FSRC, x_all, qkv_weight, [(first_own, first_fwd)], True)
    f23, f1_pair = gather(first)
    everything = [(first_own, first_fwd), (relay_own, relay_fwd), (side_own, side_fwd)]
    second = project(meta, META_SSRC, x_all, qkv_weight, everything, True)
    s23, s1_pair = gather(second)
    queries = project(meta, META_QSRC, x_all, qkv_weight, everything, False)

    w_own = lax.dynamic_slice(out_weight, (core * WB, zero), (WB, out_weight.shape[1]))
    rem_own = send(w_own, to_y)
    rem_oth = send(rem_own, to_core)

    state = attend(level0_kernel, meta, [queries[0], first[0], second[0]], STATE, ROWS)
    arrays = [queries[1], first[1], f1_pair, second[1], s1_pair, *state]
    state = attend(level1_kernel, meta, arrays, STATE, ROWS >> 1, {6: 0, 7: 1})
    arrays = [queries[2], *f23, *s23, *state]
    outs = [((TOK, WB), jnp.bfloat16)] * 2 + STATE
    att, att_send, _, _ = attend(level23_kernel, meta, arrays, outs, CUT3, {10: 2, 11: 3})
    att_oth = send(att_send, to_core)
    part = out_project(
        out_own_kernel, meta, [att, out_weight, rem_own], pltpu.VMEM((4, TOK, WB), jnp.float32), HELD, []
    )
    mixed = out_project(
        out_oth_kernel,
        meta,
        [att_oth, out_weight, rem_oth, part],
        jax.ShapeDtypeStruct((TOK, 4 * WB), jnp.bfloat16),
        FAR,
        [pltpu.VMEM((4, TOK, WB), jnp.bfloat16), pltpu.SemaphoreType.DMA((4,))],
    )
    return mixed.reshape(1, TOK, mixed.shape[1])


def solution(mesh):
    in_specs = (P("dp", "ctx", None), P(None, "dp"), P(None, "dp"), P())
    out_specs = P("dp", "ctx", None)

    return jax.shard_map(local, mesh=mesh, in_specs=in_specs, out_specs=out_specs, check_vma=False)
```

profile of v0, /device:TPU:0, one launch (start us, length us, event | category | flops | bytes accessed | tf_op | source)
XLA Modules:
  0.0 154.0 jit_solution(8891732763802484701)
XLA Ops:
  0.0 0.0 copy-start
  0.0 1.5 shard_map.46
  1.5 0.0 copy-start.1
  1.5 3.2 %collective-permute-start.1 = (bf16[1280,640]{1,0:T(8,128)(2,1)S(1)}, bf16[1280,640]{1,0:T(8,128)(2,1)}, u32[]{:S(2)}, u32[]{:S(2)}) collective-permute-start(bf16[1280,640]{1,0:T(8,128)(2,1)S(1)} %shard_map.46), channel_id=1, source_target_pairs={{0,72},{1,65},{2,74},{3,67},{4,76},{5,69},{6,78},{7,71},{64,0},{65... | collective-permute-start | bytes 4915208 | tf_op jit(solution)/shard_map/ppermute | solution.py:35
  4.7 2.6 %shard_map.47 = bf16[1280,640]{1,0:T(8,128)(2,1)} custom-call(bf16[2560,1920]{1,0:T(8,128)(2,1)} %refs_2_.5), custom_call_target="tpu_custom_call" | custom-call | tf_op jit(solution)/shard_map/pallas_call | solution.py:109
  7.3 1.0 collective-permute-start.5
  8.3 15.1 %collective-permute-done.1.refs_3_ = bf16[1280,640]{1,0:T(8,128)(2,1)} collective-permute-done((bf16[1280,640]{1,0:T(8,128)(2,1)S(1)}, bf16[1280,640]{1,0:T(8,128)(2,1)}, u32[]{:S(2)}, u32[]{:S(2)}) %collective-permute-start.1) | collective-permute-done | bytes 1638432 | tf_op jit(solution)/shard_map/ppermute | solution.py:35
  23.3 2.8 %collective-permute-start.3 = (bf16[1280,640]{1,0:T(8,128)(2,1)}, bf16[1280,640]{1,0:T(8,128)(2,1)}, u32[]{:S(2)}, u32[]{:S(2)}) collective-permute-start(bf16[1280,640]{1,0:T(8,128)(2,1)} %collective-permute-done.1.refs_3_), channel_id=1, source_target_pairs={{0,48},{1,17},{2,50},{3,19},{4,52},{5,21},{6,54},{7,23},{64,112},{... | collective-permute-start | bytes 4915208 | tf_op jit(solution)/shard_map/ppermute | solution.py:35
  26.1 0.0 collective-permute-start
  26.1 0.5 collective-permute-start.2
  26.6 14.4 %collective-permute-done.5.refs_7_ = bf16[1280,640]{1,0:T(8,128)(2,1)} collective-permute-done((bf16[1280,640]{1,0:T(8,128)(2,1)}, bf16[1280,640]{1,0:T(8,128)(2,1)}, u32[]{:S(2)}, u32[]{:S(2)}) %collective-permute-start.5) | collective-permute-done | bytes 1638432 | tf_op jit(solution)/shard_map/ppermute | solution.py:35
  41.0 0.0 collective-permute-start.6
  41.0 4.0 %collective-permute-done.3.refs_5_ = bf16[1280,640]{1,0:T(8,128)(2,1)} collective-permute-done((bf16[1280,640]{1,0:T(8,128)(2,1)}, bf16[1280,640]{1,0:T(8,128)(2,1)}, u32[]{:S(2)}, u32[]{:S(2)}) %collective-permute-start.3) | collective-permute-done | bytes 1638432 | tf_op jit(solution)/shard_map/ppermute | solution.py:35
  45.0 0.0 collective-permute-start.4
  45.0 0.0 copy-done.1
  45.0 1.3 constant_dynamic-slice_fusion
  46.3 3.8 %collective-permute-start.18 = (bf16[640,1280]{1,0:T(8,128)(2,1)}, bf16[640,1280]{1,0:T(8,128)(2,1)}, u32[]{:S(2)}, u32[]{:S(2)}) collective-permute-start(bf16[640,1280]{1,0:T(8,128)(2,1)} %constant_dynamic-slice_fusion), channel_id=1, source_target_pairs={{0,72},{1,65},{2,74},{3,67},{4,76},{5,69},{6,78},{7,71},{64,0},{65... | collective-permute-start | bytes 4915208 | tf_op jit(solution)/shard_map/ppermute | solution.py:35
  50.1 0.0 copy-done
  50.1 0.1 constant_dynamic-slice_fusion.1
  50.2 0.1 reshape.9
  50.3 0.1 concatenate.3.refs_0_.meta
  50.4 0.0 collective-permute-done.x_oth
  50.4 2.2 %stage.1.refs_1_ = bf16[768,2560]{1,0:T(8,128)(2,1)S(1)} custom-call(bf16[384,2560]{1,0:T(8,128)(2,1)} %bitcast.8.x_own, bf16[384,2560]{1,0:T(8,128)(2,1)} %collective-permute-done.x_oth), custom_call_target="tpu_custom_call" | custom-call | tf_op jit(solution)/shard_map/stage/pallas_call | solution.py:88
  52.5 0.0 collective-permute-done.2.refs_4_
  52.5 5.5 %shard_map.49 = (bf16[768,640]{1,0:T(8,128)(2,1)S(1)}, bf16[384,640]{1,0:T(8,128)(2,1)S(1)}, bf16[384,640]{1,0:T(8,128)(2,1)S(1)}, bf16[96,640]{1,0:T(8,128)(2,1)S(1)}) custom-call(s32[36]{0:T(128)S(1)} %concatenate.3.refs_0_.meta, bf16[768,2560]{1,0:T(8,128)(2,1)S(1)} %stage.1.refs_1_, bf16[2560,1920]{1,0:T(8,128)(2,1)} %refs_2_.5, ...), custom_call_target="tpu_custom_call" | custom-call | flops 2516582400 | bytes 9175040 | tf_op jit(solution)/shard_map/pallas_call | solution.py:181
  58.0 0.1 collective-permute-start.7
  58.1 0.0 collective-permute-done.6.refs_8_
  58.2 0.0 collective-permute-done.4.refs_6_
  58.2 5.5 %shard_map.50 = (bf16[768,640]{1,0:T(8,128)(2,1)S(1)}, bf16[384,640]{1,0:T(8,128)(2,1)S(1)}, bf16[384,640]{1,0:T(8,128)(2,1)S(1)}, bf16[96,640]{1,0:T(8,128)(2,1)S(1)}) custom-call(s32[36]{0:T(128)S(1)} %concatenate.3.refs_0_.meta, bf16[768,2560]{1,0:T(8,128)(2,1)S(1)} %stage.1.refs_1_, bf16[2560,1920]{1,0:T(8,128)(2,1)} %refs_2_.5, ...), custom_call_target="tpu_custom_call" | custom-call | flops 2516582400 | bytes 9175040 | tf_op jit(solution)/shard_map/pallas_call | solution.py:181
  63.7 3.6 %collective-permute-start.11 = (bf16[96,640]{1,0:T(8,128)(2,1)S(1)}, bf16[96,640]{1,0:T(8,128)(2,1)S(1)}, u32[]{:S(2)}, u32[]{:S(2)}) collective-permute-start(bf16[96,640]{1,0:T(8,128)(2,1)S(1)} %get-tuple-element.26), channel_id=1, source_target_pairs={{0,8},{1,9},{2,10},{3,11},{4,12},{5,13},{6,14},{7,15},{64,72},{65,... | collective-permute-start | bytes 368648 | tf_op jit(solution)/shard_map/ppermute | solution.py:35
  67.3 7.1 %collective-permute-done.18.rem = bf16[640,1280]{1,0:T(8,128)(2,1)} collective-permute-done((bf16[640,1280]{1,0:T(8,128)(2,1)}, bf16[640,1280]{1,0:T(8,128)(2,1)}, u32[]{:S(2)}, u32[]{:S(2)}) %collective-permute-start.18) | collective-permute-done | bytes 1638432 | tf_op jit(solution)/shard_map/ppermute | solution.py:35
  74.3 0.0 collective-permute-start.19
  74.3 1.9 %collective-permute-start.15 = (bf16[384,640]{1,0:T(8,128)(2,1)S(1)}, bf16[384,640]{1,0:T(8,128)(2,1)S(1)}, u32[]{:S(2)}, u32[]{:S(2)}) collective-permute-start(bf16[384,640]{1,0:T(8,128)(2,1)S(1)} %get-tuple-element.28.refs_2_), channel_id=1, source_target_pairs={{0,2},{1,3},{2,0},{3,1},{4,6},{5,7},{6,4},{7,5},{64,66},{65,67},{6... | collective-permute-start | bytes 1474568 | tf_op jit(solution)/shard_map/ppermute | solution.py:35
  76.2 0.0 collective-permute-done.7
  76.3 0.2 collective-permute-start.8
  76.4 1.9 %collective-permute-start.16 = (bf16[384,640]{1,0:T(8,128)(2,1)S(1)}, bf16[384,640]{1,0:T(8,128)(2,1)S(1)}, u32[]{:S(2)}, u32[]{:S(2)}) collective-permute-start(bf16[384,640]{1,0:T(8,128)(2,1)S(1)} %get-tuple-element.29.refs_4_), channel_id=1, source_target_pairs={{0,2},{1,3},{2,0},{3,1},{4,6},{5,7},{6,4},{7,5},{64,66},{65,67},{6... | collective-permute-start | bytes 1474568 | tf_op jit(solution)/shard_map/ppermute | solution.py:35
  78.4 0.0 collective-permute-done.11
  78.4 0.2 collective-permute-start.12
  78.6 9.8 %collective-permute-done.15.refs_3_ = bf16[384,640]{1,0:T(8,128)(2,1)S(1)} collective-permute-done((bf16[384,640]{1,0:T(8,128)(2,1)S(1)}, bf16[384,640]{1,0:T(8,128)(2,1)S(1)}, u32[]{:S(2)}, u32[]{:S(2)}) %collective-permute-start.15) | collective-permute-done | bytes 491552 | tf_op jit(solution)/shard_map/ppermute | solution.py:35
  88.4 4.0 %collective-permute-start.9 = (bf16[384,640]{1,0:T(8,128)(2,1)S(1)}, bf16[384,640]{1,0:T(8,128)(2,1)S(1)}, u32[]{:S(2)}, u32[]{:S(2)}) collective-permute-start(bf16[384,640]{1,0:T(8,128)(2,1)S(1)} %constant_dynamic-update-slice_fusion.1.refs_2_), channel_id=1, source_target_pairs={{0,6},{1,7},{2,4},{3,5},{4,2},{5,3},{6,0},{7,1},{64,70},{65,71},{6... | collective-permute-start | bytes 1474568 | tf_op jit(solution)/shard_map/ppermute | solution.py:35
  92.5 6.5 %collective-permute-done.8.refs_3_ = bf16[384,640]{1,0:T(8,128)(2,1)S(1)} collective-permute-done((bf16[384,640]{1,0:T(8,128)(2,1)S(1)}, bf16[384,640]{1,0:T(8,128)(2,1)S(1)}, u32[]{:S(2)}, u32[]{:S(2)}) %collective-permute-start.8) | collective-permute-done | bytes 491552 | tf_op jit(solution)/shard_map/ppermute | solution.py:35
  98.9 4.0 %collective-permute-start.10 = (bf16[384,640]{1,0:T(8,128)(2,1)S(1)}, bf16[384,640]{1,0:T(8,128)(2,1)S(1)}, u32[]{:S(2)}, u32[]{:S(2)}) collective-permute-start(bf16[384,640]{1,0:T(8,128)(2,1)S(1)} %collective-permute-done.8.refs_3_), channel_id=1, source_target_pairs={{0,6},{1,7},{2,4},{3,5},{4,2},{5,3},{6,0},{7,1},{64,70},{65,71},{6... | collective-permute-start | bytes 1474568 | tf_op jit(solution)/shard_map/ppermute | solution.py:35
  103.0 6.5 %collective-permute-done.16.refs_5_ = bf16[384,640]{1,0:T(8,128)(2,1)S(1)} collective-permute-done((bf16[384,640]{1,0:T(8,128)(2,1)S(1)}, bf16[384,640]{1,0:T(8,128)(2,1)S(1)}, u32[]{:S(2)}, u32[]{:S(2)}) %collective-permute-start.16) | collective-permute-done | bytes 491552 | tf_op jit(solution)/shard_map/ppermute | solution.py:35
  109.5 4.0 %collective-permute-start.13 = (bf16[384,640]{1,0:T(8,128)(2,1)S(1)}, bf16[384,640]{1,0:T(8,128)(2,1)S(1)}, u32[]{:S(2)}, u32[]{:S(2)}) collective-permute-start(bf16[384,640]{1,0:T(8,128)(2,1)S(1)} %constant_dynamic-update-slice_fusion.refs_6_), channel_id=1, source_target_pairs={{0,6},{1,7},{2,4},{3,5},{4,2},{5,3},{6,0},{7,1},{64,70},{65,71},{6... | collective-permute-start | bytes 1474568 | tf_op jit(solution)/shard_map/ppermute | solution.py:35
  113.5 6.2 %collective-permute-done.12.refs_7_ = bf16[384,640]{1,0:T(8,128)(2,1)S(1)} collective-permute-done((bf16[384,640]{1,0:T(8,128)(2,1)S(1)}, bf16[384,640]{1,0:T(8,128)(2,1)S(1)}, u32[]{:S(2)}, u32[]{:S(2)}) %collective-permute-start.12) | collective-permute-done | bytes 491552 | tf_op jit(solution)/shard_map/ppermute | solution.py:35
  119.7 3.9 %collective-permute-start.14 = (bf16[384,640]{1,0:T(8,128)(2,1)S(1)}, bf16[384,640]{1,0:T(8,128)(2,1)S(1)}, u32[]{:S(2)}, u32[]{:S(2)}) collective-permute-start(bf16[384,640]{1,0:T(8,128)(2,1)S(1)} %collective-permute-done.12.refs_7_), channel_id=1, source_target_pairs={{0,6},{1,7},{2,4},{3,5},{4,2},{5,3},{6,0},{7,1},{64,70},{65,71},{6... | collective-permute-start | bytes 1474568 | tf_op jit(solution)/shard_map/ppermute | solution.py:35
  123.6 5.5 %shard_map.48 = (bf16[768,640]{1,0:T(8,128)(2,1)S(1)}, bf16[384,640]{1,0:T(8,128)(2,1)S(1)}, bf16[288,640]{1,0:T(8,128)(2,1)S(1)}) custom-call(s32[36]{0:T(128)S(1)} %concatenate.3.refs_0_.meta, bf16[768,2560]{1,0:T(8,128)(2,1)S(1)} %stage.1.refs_1_, bf16[2560,1920]{1,0:T(8,128)(2,1)} %refs_2_.5, bf16[1280,640]{1,0:T(8,128)(2,1)} %collective-permute-done.1.refs_3_, ...), custom_call_target="tpu_custom_call" | custom-call | flops 2516582400 | bytes 9175040 | tf_op jit(solution)/shard_map/pallas_call | solution.py:181
  129.1 4.7 %shard_map.51 = (f32[5,768,128]{2,1,0:T(8,128)S(1)}, f32[5,768,128]{2,1,0:T(8,128)S(1)}) custom-call(s32[36]{0:T(128)S(1)} %concatenate.3.refs_0_.meta, bf16[768,640]{1,0:T(8,128)(2,1)S(1)} %get-tuple-element.30.refs_1_, bf16[768,640]{1,0:T(8,128)(2,1)S(1)} %get-tuple-element.31.refs_2_, bf16[768,640]{1,0:T(8,128)(2,1)S(1)} %get-tuple-element.32.refs_3_), custom_call_target="tpu_custom_call" | custom-call | flops 1509949440 | bytes 2949120 | tf_op jit(solution)/shard_map/pallas_call | solution.py:271
  133.8 5.7 %shard_map.52 = (f32[5,768,128]{2,1,0:T(8,128)S(1)}, f32[5,768,128]{2,1,0:T(8,128)S(1)}) custom-call(s32[36]{0:T(128)S(1)} %concatenate.3.refs_0_.meta, bf16[384,640]{1,0:T(8,128)(2,1)S(1)} %get-tuple-element.27.refs_1_, bf16[384,640]{1,0:T(8,128)(2,1)S(1)} %get-tuple-element.28.refs_2_, ...), custom_call_target="tpu_custom_call", output_to_operand_aliasing={{0}: (6, {}), {1}: (7, {})} | custom-call | flops 754974720 | bytes 2457600 | tf_op jit(solution)/shard_map/pallas_call | solution.py:271
  139.5 0.0 collective-permute-done.9.refs_4_
  139.5 0.0 collective-permute-done.10.refs_5_
  139.5 0.0 collective-permute-done.13.refs_8_
  139.5 0.0 collective-permute-done.14.refs_9_
  139.5 7.4 %shard_map.53 = (bf16[384,640]{1,0:T(8,128)(2,1)S(1)}, bf16[384,640]{1,0:T(8,128)(2,1)S(1)}, f32[5,768,128]{2,1,0:T(8,128)S(1)}, f32[5,768,128]{2,1,0:T(8,128)S(1)}) custom-call(s32[36]{0:T(128)S(1)} %concatenate.3.refs_0_.meta, bf16[288,640]{1,0:T(8,128)(2,1)S(1)} %get-tuple-element.22.refs_1_, ...), custom_call_target="tpu_custom_call", output_to_operand_aliasing={{2}: (10, {}), {3}: (11, {})} | custom-call | flops 566231040 | bytes 2334720 | tf_op jit(solution)/shard_map/pallas_call | solution.py:271
  147.0 0.1 collective-permute-start.17
  147.1 3.4 %shard_map.54.part = f32[4,384,640]{2,1,0:T(8,128)S(1)} custom-call(s32[36]{0:T(128)S(1)} %concatenate.3.refs_0_.meta, bf16[384,640]{1,0:T(8,128)(2,1)S(1)} %get-tuple-element.38.att, bf16[1280,1280]{1,0:T(8,128)(2,1)S(1)} %copy-done.1, bf16[640,1280]{1,0:T(8,128)(2,1)} %collective-permute-done.18.rem), custom_call_target="tpu_custom_call" | custom-call | flops 1258291200 | bytes 5242880 | tf_op jit(solution)/shard_map/pallas_call | solution.py:310
  150.4 0.0 collective-permute-done.19.rem
  150.5 0.0 collective-permute-done.17.att
  150.5 3.3 %shard_map.55 = bf16[384,2560]{1,0:T(8,128)(2,1)} custom-call(s32[36]{0:T(128)S(1)} %concatenate.3.refs_0_.meta, bf16[384,640]{1,0:T(8,128)(2,1)S(1)} %collective-permute-done.17.att, bf16[1280,1280]{1,0:T(8,128)(2,1)S(1)} %copy-done.1, bf16[640,1280]{1,0:T(8,128)(2,1)S(1)} %collective-permute-done.19.rem, f32[4,384,640]{2,1,0:T(8,128)S(1)} %shard_map.54.part), custom_call_target="tpu_custom_call" | custom-call | flops 1258291200 | bytes 5242880 | tf_op jit(solution)/shard_map/pallas_call | solution.py:310
  (4 shorter events, 0.0 us)
Async XLA Ops:
  0.0 50.1 %copy-start = (s32[4,10]{1,0:T(4,128)S(1)}, s32[4,10]{1,0:T(4,128)}, u32[]{:S(2)}) copy-start(s32[4,10]{1,0:T(4,128)} %param.7) | copy-start | bytes 484
  1.5 43.6 %copy-start.1 = (bf16[1280,1280]{1,0:T(8,128)(2,1)S(1)}, bf16[1280,1280]{1,0:T(8,128)(2,1)}, u32[]{:S(2)}) copy-start(bf16[1280,1280]{1,0:T(8,128)(2,1)} %w_loc.3) | copy-start | bytes 9830404
  1.5 21.8 %collective-permute-start.1 = (bf16[1280,640]{1,0:T(8,128)(2,1)S(1)}, bf16[1280,640]{1,0:T(8,128)(2,1)}, u32[]{:S(2)}, u32[]{:S(2)}) collective-permute-start(bf16[1280,640]{1,0:T(8,128)(2,1)S(1)} %shard_map.46), channel_id=1, source_target_pairs={{0,72},{1,65},{2,74},{3,67},{4,76},{5,69},{6,78},{7,71},{64,0},{65... | collective-permute-start | bytes 4915208 | tf_op jit(solution)/shard_map/ppermute | solution.py:35
  7.3 33.7 %collective-permute-start.5 = (bf16[1280,640]{1,0:T(8,128)(2,1)}, bf16[1280,640]{1,0:T(8,128)(2,1)}, u32[]{:S(2)}, u32[]{:S(2)}) collective-permute-start(bf16[1280,640]{1,0:T(8,128)(2,1)} %shard_map.47), channel_id=1, source_target_pairs={{0,72},{1,65},{2,74},{3,67},{4,76},{5,69},{6,78},{7,71},{64,0},{65... | collective-permute-start | bytes 4915208 | tf_op jit(solution)/shard_map/ppermute | solution.py:35
  23.3 21.7 %collective-permute-start.3 = (bf16[1280,640]{1,0:T(8,128)(2,1)}, bf16[1280,640]{1,0:T(8,128)(2,1)}, u32[]{:S(2)}, u32[]{:S(2)}) collective-permute-start(bf16[1280,640]{1,0:T(8,128)(2,1)} %collective-permute-done.1.refs_3_), channel_id=1, source_target_pairs={{0,48},{1,17},{2,50},{3,19},{4,52},{5,21},{6,54},{7,23},{64,112},{... | collective-permute-start | bytes 4915208 | tf_op jit(solution)/shard_map/ppermute | solution.py:35
  26.1 24.3 %collective-permute-start = (bf16[384,2560]{1,0:T(8,128)(2,1)}, bf16[384,2560]{1,0:T(8,128)(2,1)}, u32[]{:S(2)}, u32[]{:S(2)}) collective-permute-start(bf16[384,2560]{1,0:T(8,128)(2,1)} %bitcast.8.x_own), channel_id=1, source_target_pairs={{0,1},{1,0},{2,3},{3,2},{4,5},{5,4},{6,7},{7,6},{64,65},{65,64},{6... | collective-permute-start | bytes 5898248 | tf_op jit(solution)/shard_map/ppermute | solution.py:35
  26.1 26.5 %collective-permute-start.2 = (bf16[1280,640]{1,0:T(8,128)(2,1)}, bf16[1280,640]{1,0:T(8,128)(2,1)}, u32[]{:S(2)}, u32[]{:S(2)}) collective-permute-start(bf16[1280,640]{1,0:T(8,128)(2,1)} %collective-permute-done.1.refs_3_), channel_id=1, source_target_pairs={{0,1},{1,0},{2,3},{3,2},{4,5},{5,4},{6,7},{7,6},{64,65},{65,64},{6... | collective-permute-start | bytes 4915208 | tf_op jit(solution)/shard_map/ppermute | solution.py:35
  41.0 17.2 %collective-permute-start.6 = (bf16[1280,640]{1,0:T(8,128)(2,1)}, bf16[1280,640]{1,0:T(8,128)(2,1)}, u32[]{:S(2)}, u32[]{:S(2)}) collective-permute-start(bf16[1280,640]{1,0:T(8,128)(2,1)} %collective-permute-done.5.refs_7_), channel_id=1, source_target_pairs={{0,1},{1,0},{2,3},{3,2},{4,5},{5,4},{6,7},{7,6},{64,65},{65,64},{6... | collective-permute-start | bytes 4915208 | tf_op jit(solution)/shard_map/ppermute | solution.py:35
  45.0 13.1 %collective-permute-start.4 = (bf16[1280,640]{1,0:T(8,128)(2,1)}, bf16[1280,640]{1,0:T(8,128)(2,1)}, u32[]{:S(2)}, u32[]{:S(2)}) collective-permute-start(bf16[1280,640]{1,0:T(8,128)(2,1)} %collective-permute-done.3.refs_5_), channel_id=1, source_target_pairs={{0,1},{1,0},{2,3},{3,2},{4,5},{5,4},{6,7},{7,6},{64,65},{65,64},{6... | collective-permute-start | bytes 4915208 | tf_op jit(solution)/shard_map/ppermute | solution.py:35
  46.3 28.0 %collective-permute-start.18 = (bf16[640,1280]{1,0:T(8,128)(2,1)}, bf16[640,1280]{1,0:T(8,128)(2,1)}, u32[]{:S(2)}, u32[]{:S(2)}) collective-permute-start(bf16[640,1280]{1,0:T(8,128)(2,1)} %constant_dynamic-slice_fusion), channel_id=1, source_target_pairs={{0,72},{1,65},{2,74},{3,67},{4,76},{5,69},{6,78},{7,71},{64,0},{65... | collective-permute-start | bytes 4915208 | tf_op jit(solution)/shard_map/ppermute | solution.py:35
  58.0 18.2 %collective-permute-start.7 = (bf16[96,640]{1,0:T(8,128)(2,1)S(1)}, bf16[96,640]{1,0:T(8,128)(2,1)S(1)}, u32[]{:S(2)}, u32[]{:S(2)}) collective-permute-start(bf16[96,640]{1,0:T(8,128)(2,1)S(1)} %get-tuple-element.24), channel_id=1, source_target_pairs={{0,8},{1,9},{2,10},{3,11},{4,12},{5,13},{6,14},{7,15},{64,72},{65,... | collective-permute-start | bytes 368648 | tf_op jit(solution)/shard_map/ppermute | solution.py:35
  63.7 14.7 %collective-permute-start.11 = (bf16[96,640]{1,0:T(8,128)(2,1)S(1)}, bf16[96,640]{1,0:T(8,128)(2,1)S(1)}, u32[]{:S(2)}, u32[]{:S(2)}) collective-permute-start(bf16[96,640]{1,0:T(8,128)(2,1)S(1)} %get-tuple-element.26), channel_id=1, source_target_pairs={{0,8},{1,9},{2,10},{3,11},{4,12},{5,13},{6,14},{7,15},{64,72},{65,... | collective-permute-start | bytes 368648 | tf_op jit(solution)/shard_map/ppermute | solution.py:35
  74.3 76.1 %collective-permute-start.19 = (bf16[640,1280]{1,0:T(8,128)(2,1)}, bf16[640,1280]{1,0:T(8,128)(2,1)S(1)}, u32[]{:S(2)}, u32[]{:S(2)}) collective-permute-start(bf16[640,1280]{1,0:T(8,128)(2,1)} %collective-permute-done.18.rem), channel_id=1, source_target_pairs={{0,1},{1,0},{2,3},{3,2},{4,5},{5,4},{6,7},{7,6},{64,65},{65,64},{6... | collective-permute-start | bytes 4915208 | tf_op jit(solution)/shard_map/ppermute | solution.py:35
  74.3 14.1 %collective-permute-start.15 = (bf16[384,640]{1,0:T(8,128)(2,1)S(1)}, bf16[384,640]{1,0:T(8,128)(2,1)S(1)}, u32[]{:S(2)}, u32[]{:S(2)}) collective-permute-start(bf16[384,640]{1,0:T(8,128)(2,1)S(1)} %get-tuple-element.28.refs_2_), channel_id=1, source_target_pairs={{0,2},{1,3},{2,0},{3,1},{4,6},{5,7},{6,4},{7,5},{64,66},{65,67},{6... | collective-permute-start | bytes 1474568 | tf_op jit(solution)/shard_map/ppermute | solution.py:35
  76.3 22.7 %collective-permute-start.8 = (bf16[384,640]{1,0:T(8,128)(2,1)S(1)}, bf16[384,640]{1,0:T(8,128)(2,1)S(1)}, u32[]{:S(2)}, u32[]{:S(2)}) collective-permute-start(bf16[384,640]{1,0:T(8,128)(2,1)S(1)} %constant_dynamic-update-slice_fusion.1.refs_2_), channel_id=1, source_target_pairs={{0,2},{1,3},{2,0},{3,1},{4,6},{5,7},{6,4},{7,5},{64,66},{65,67},{6... | collective-permute-start | bytes 1474568 | tf_op jit(solution)/shard_map/ppermute | solution.py:35
  76.4 33.0 %collective-permute-start.16 = (bf16[384,640]{1,0:T(8,128)(2,1)S(1)}, bf16[384,640]{1,0:T(8,128)(2,1)S(1)}, u32[]{:S(2)}, u32[]{:S(2)}) collective-permute-start(bf16[384,640]{1,0:T(8,128)(2,1)S(1)} %get-tuple-element.29.refs_4_), channel_id=1, source_target_pairs={{0,2},{1,3},{2,0},{3,1},{4,6},{5,7},{6,4},{7,5},{64,66},{65,67},{6... | collective-permute-start | bytes 1474568 | tf_op jit(solution)/shard_map/ppermute | solution.py:35
  78.4 41.3 %collective-permute-start.12 = (bf16[384,640]{1,0:T(8,128)(2,1)S(1)}, bf16[384,640]{1,0:T(8,128)(2,1)S(1)}, u32[]{:S(2)}, u32[]{:S(2)}) collective-permute-start(bf16[384,640]{1,0:T(8,128)(2,1)S(1)} %constant_dynamic-update-slice_fusion.refs_6_), channel_id=1, source_target_pairs={{0,2},{1,3},{2,0},{3,1},{4,6},{5,7},{6,4},{7,5},{64,66},{65,67},{6... | collective-permute-start | bytes 1474568 | tf_op jit(solution)/shard_map/ppermute | solution.py:35
  88.4 51.1 %collective-permute-start.9 = (bf16[384,640]{1,0:T(8,128)(2,1)S(1)}, bf16[384,640]{1,0:T(8,128)(2,1)S(1)}, u32[]{:S(2)}, u32[]{:S(2)}) collective-permute-start(bf16[384,640]{1,0:T(8,128)(2,1)S(1)} %constant_dynamic-update-slice_fusion.1.refs_2_), channel_id=1, source_target_pairs={{0,6},{1,7},{2,4},{3,5},{4,2},{5,3},{6,0},{7,1},{64,70},{65,71},{6... | collective-permute-start | bytes 1474568 | tf_op jit(solution)/shard_map/ppermute | solution.py:35
  98.9 40.6 %collective-permute-start.10 = (bf16[384,640]{1,0:T(8,128)(2,1)S(1)}, bf16[384,640]{1,0:T(8,128)(2,1)S(1)}, u32[]{:S(2)}, u32[]{:S(2)}) collective-permute-start(bf16[384,640]{1,0:T(8,128)(2,1)S(1)} %collective-permute-done.8.refs_3_), channel_id=1, source_target_pairs={{0,6},{1,7},{2,4},{3,5},{4,2},{5,3},{6,0},{7,1},{64,70},{65,71},{6... | collective-permute-start | bytes 1474568 | tf_op jit(solution)/shard_map/ppermute | solution.py:35
  109.5 30.1 %collective-permute-start.13 = (bf16[384,640]{1,0:T(8,128)(2,1)S(1)}, bf16[384,640]{1,0:T(8,128)(2,1)S(1)}, u32[]{:S(2)}, u32[]{:S(2)}) collective-permute-start(bf16[384,640]{1,0:T(8,128)(2,1)S(1)} %constant_dynamic-update-slice_fusion.refs_6_), channel_id=1, source_target_pairs={{0,6},{1,7},{2,4},{3,5},{4,2},{5,3},{6,0},{7,1},{64,70},{65,71},{6... | collective-permute-start | bytes 1474568 | tf_op jit(solution)/shard_map/ppermute | solution.py:35
  119.7 19.8 %collective-permute-start.14 = (bf16[384,640]{1,0:T(8,128)(2,1)S(1)}, bf16[384,640]{1,0:T(8,128)(2,1)S(1)}, u32[]{:S(2)}, u32[]{:S(2)}) collective-permute-start(bf16[384,640]{1,0:T(8,128)(2,1)S(1)} %collective-permute-done.12.refs_7_), channel_id=1, source_target_pairs={{0,6},{1,7},{2,4},{3,5},{4,2},{5,3},{6,0},{7,1},{64,70},{65,71},{6... | collective-permute-start | bytes 1474568 | tf_op jit(solution)/shard_map/ppermute | solution.py:35
  147.0 3.5 %collective-permute-start.17 = (bf16[384,640]{1,0:T(8,128)(2,1)S(1)}, bf16[384,640]{1,0:T(8,128)(2,1)S(1)}, u32[]{:S(2)}, u32[]{:S(2)}) collective-permute-start(bf16[384,640]{1,0:T(8,128)(2,1)S(1)} %get-tuple-element.37), channel_id=1, source_target_pairs={{0,1},{1,0},{2,3},{3,2},{4,5},{5,4},{6,7},{7,6},{64,65},{65,64},{6... | collective-permute-start | bytes 1474568 | tf_op jit(solution)/shard_map/ppermute | solution.py:35
where the time goes:
time: 156 us; the launch traced here: 154 us
  waiting for transfers between devices  69.6 us (45%)
  Pallas kernels  47.2 us (30%)
  starting transfers between devices  35.2 us (23%)
  local copies, waits for them, and re-layouts  1.57 us (1%)
    ppermute x20, waiting for transfers between devices, send(): return lax.ppermute(block, ('dp', 'ctx'), route)  69.6 us
    ppermute x20, starting transfers between devices, send(): return lax.ppermute(block, ('dp', 'ctx'), route)  35.2 us
    pallas_call x3, Pallas kernels, attend(): pl.pallas_call(lambda *refs: kernel(factor, *refs), out_shape=[pltpu.VMEM...  17.8 us
    pallas_call x3, Pallas kernels, project(): pl.pallas_call(lambda *refs: proj_kernel(len(remotes), slot, for_keys, *r...  16.5 us
    pallas_call x2, Pallas kernels, out_project(): pl.pallas_call(kernel, out_shape=out_shape, in_specs=[SCALARS] + [HELD] *...  6.69 us
    pallas_call x2, Pallas kernels, payload(): pl.pallas_call(lambda *refs: payload_kernel(block, *refs), out_shape=pltp...  4.05 us
  transfers between devices with their start and end apart: 20, of which 8 were waited for; matrix products, arithmetic and copies ran while one was open for 1% of the time, Pallas kernels for 28%

commit v1 on v0

--- a/solution.py
+++ b/solution.py
@@ -15,7 +15,7 @@
 KC = 1280
 LOG2E = 1.4426950408889634
 
-META_CORE, META_FSRC, _, META_SSRC, _, META_QSRC, _, META_FK, META_DP = range(9)
+META_CORE, META_FSRC, META_FBLK, META_SSRC, META_SBLK, META_QSRC, META_QBLK, META_FK, META_DP = range(9)
 META_OFF = 16
 
 
@@ -76,6 +76,32 @@
     return pltpu.CompilerParams(vmem_limit_bytes=mib << 20)
 
 
+def scalars_kernel(offsets, meta):
+    d = lax.axis_index("dp")
+    ctx = lax.axis_index("ctx")
+    core = lax.rem(ctx, 2)
+    odd = lax.rem(ctx // 16, 2)
+    place = 2 * d + core
+
+    def pick(*by_place):
+        got = jnp.int32(by_place[3])
+        for n in range(3):
+            got = jnp.where(place == n, by_place[n], got)
+        return got
+
+    meta[META_CORE] = core
+    meta[META_DP] = d
+    meta[META_FSRC], meta[META_FBLK] = pick(0, 1, 0, 0), pick(2, 0, 1, 0)
+    meta[META_SSRC], meta[META_SBLK] = pick(3, 2, 1 + odd, 0), pick(0, 0, 0, 2)
+    meta[META_QSRC], meta[META_QBLK] = pick(0, 0, 2 - odd, 3), pick(0, 1, 0, 0)
+    meta[META_FK] = pick(1, 1 - odd, 0, 1)
+    for n in range(9, META_OFF):
+        meta[n] = 0
+    for j in range(LEVELS):
+        for h in range(HH):
+            meta[META_OFF + j * HH + h] = jnp.where(core == 0, offsets[j, h], offsets[j, HH + h])
+
+
 def stage_kernel(x_own, x_oth, x_all, sem):
     copies = [pltpu.make_async_copy(x, x_all.at[pl.ds(g * TOK, TOK)], sem.at[g]) for g, x in enumerate((x_own, x_oth))]
     for copy in copies:
@@ -96,11 +122,42 @@
     )(*far(x_own, x_oth))
 
 
+def join_kernel(far_rows, _block, out):
+    out[pl.ds(CUT3, ROWS >> 3), :] = far_rows[...]
+
+
+def join(block, far_rows):
+    return pl.pallas_call(
+        join_kernel,
+        out_shape=pltpu.VMEM(block.shape, block.dtype),
+        in_specs=[HELD, HELD],
+        out_specs=HELD,
+        input_output_aliases={1: 0},
+        compiler_params=params(3),
+    )(*held(far_rows, block))
+
+
+def collect_kernel(*refs):
+    for n, ref in enumerate(refs[:-1]):
+        refs[-1][pl.ds(n * (ROWS >> 3), ROWS >> 3), :] = ref[pl.ds(CUT2, ROWS >> 3), :]
+
+
+def collect(blocks):
+    return pl.pallas_call(
+        collect_kernel,
+        out_shape=pltpu.VMEM((len(blocks) * (ROWS >> 3), WB), blocks[0].dtype),
+        in_specs=[HELD] * len(blocks),
+        out_specs=HELD,
+        compiler_params=params(3),
+    )(*held(*blocks))
+
+
 def payload_kernel(block, w, out, sem):
-    core = lax.axis_index("ctx") % 2
+    core = lax.rem(lax.axis_index("ctx"), 2)
     half = w.shape[0] // 2
     rows = pl.ds(pl.multiple_of(core * half, half), half)
-    copy = pltpu.make_async_copy(w.at[rows, pl.ds(pl.multiple_of(block() * WB, HD), WB)], out, sem.at[0])
+    source = w.at[rows] if block is None else w.at[rows, pl.ds(pl.multiple_of(block() * WB, HD), WB)]
+    copy = pltpu.make_async_copy(source, out, sem.at[0])
     copy.start()
     copy.wait()
 
@@ -108,7 +165,7 @@
 def payload(block, w):
     return pl.pallas_call(
         lambda *refs: payload_kernel(block, *refs),
-        out_shape=pltpu.VMEM((w.shape[0] // 2, WB), w.dtype),
+        out_shape=pltpu.VMEM((w.shape[0] // 2, w.shape[1] if block is None else WB), w.dtype),
         in_specs=[FAR],
         out_specs=HELD,
         scratch_shapes=[pltpu.SemaphoreType.DMA((1,))],
@@ -181,7 +238,7 @@
     return pl.pallas_call(
         lambda *refs: proj_kernel(len(remotes), slot, for_keys, *refs),
         out_shape=[pltpu.VMEM(s, jnp.bfloat16) for s in shapes],
-        in_specs=[SCALARS, HELD] + [FAR] * (1 + len(flat)),
+        in_specs=[SCALARS, HELD, FAR] + [HELD] * len(flat),
         out_specs=[HELD] * len(shapes),
         scratch_shapes=[
             pltpu.VMEM((depth, WB), jnp.bfloat16),
@@ -192,7 +249,7 @@
         cost_estimate=pl.CostEstimate(
             flops=2 * ROWS * depth * WB, transcendentals=0, bytes_accessed=2 * (ROWS * depth + depth * WB + 2 * ROWS * WB)
         ),
-    )(meta, *held(x_all), *far(w_loc, *flat))
+    )(meta, *held(x_all), *far(w_loc), *held(*flat))
 
 
 def softmax_rows(q, keys, values, factor):
@@ -222,20 +279,17 @@
     ml_ref[where] = pack(newest, old_total * former + total * fresh)
 
 
-def choose(meta, firsts, seconds, cut, cols):
+def choose(meta, firsts, seconds):
     f_is_k = jnp.full((1, 1), meta[META_FK], jnp.int32) == 1
-    keys, values = [], []
-    for f_ref, s_ref in zip(firsts, seconds):
-        f, s = f_ref[cut, cols], s_ref[cut, cols]
-        keys.append(jnp.where(f_is_k, f, s))
-        values.append(jnp.where(f_is_k, s, f))
-    return keys, values
+    f = firsts[0] if len(firsts) == 1 else jnp.concatenate(firsts, axis=0)
+    s = seconds[0] if len(seconds) == 1 else jnp.concatenate(seconds, axis=0)
+    return [jnp.where(f_is_k, f, s)], [jnp.where(f_is_k, s, f)]
 
 
 def level0_kernel(factor, meta, q_ref, f_ref, s_ref, acc_ref, ml_ref):
     for h in range(HH):
         cols = pl.ds(h * HD, HD)
-        keys, values = choose(meta, [f_ref], [s_ref], slice(None), cols)
+        keys, values = choose(meta, [f_ref[:, cols]], [s_ref[:, cols]])
         for start in range(0, ROWS, TOK):
             blend, top, total = softmax_rows(q_ref[pl.ds(start, TOK), cols], keys, values, factor)
             acc_ref[h, pl.ds(start, TOK), :] = blend
@@ -245,17 +299,23 @@
 def level1_kernel(factor, meta, q_ref, f0, f1, s0, s1, _acc, _ml, acc_ref, ml_ref):
     for h in range(HH):
         cols = pl.ds(h * HD, HD)
-        keys, values = choose(meta, [f0, f1], [s0, s1], slice(None), cols)
+        keys, values = choose(meta, [f0[:, cols], f1[:, cols]], [s0[:, cols], s1[:, cols]])
         where = (h, pl.ds(meta[META_OFF + HH + h], TOK, stride=2), slice(None))
         merge(acc_ref, ml_ref, where, *softmax_rows(q_ref[:, cols], keys, values, factor))
 
 
-def level23_kernel(factor, meta, q_ref, f0, f1, f2, f3, s0, s1, s2, s3, _acc, _ml, own_ref, oth_ref, acc, ml):
+def level23_kernel(factor, meta, q_ref, *refs):
+    fs, f_far, ss, (own_ref, oth_ref, acc, ml) = refs[:4], refs[4], refs[5:9], refs[11:]
+    third = ROWS >> 3
     for h in range(HH):
         cols = pl.ds(h * HD, HD)
-        for level, low, rows in ((2, 0, CUT2), (3, CUT2, ROWS >> 3)):
-            cut = slice(0, CUT2) if level == 2 else slice(CUT2, ROWS >> 1)
-            keys, values = choose(meta, [f0, f1, f2, f3], [s0, s1, s2, s3], cut, cols)
+        for level, low, rows in ((2, 0, CUT2), (3, CUT2, third)):
+            if level == 2:
+                firsts, seconds = [f[:CUT2, cols] for f in fs], [s[:CUT2, cols] for s in ss]
+            else:
+                firsts = [r for n, f in enumerate(fs) for r in (f[CUT2:, cols], f_far[pl.ds(n * third, third), cols])]
+                seconds = [s[CUT2:, cols] for s in ss]
+            keys, values = choose(meta, firsts, seconds)
             where = (h, pl.ds(meta[META_OFF + level * HH + h], rows, stride=1 << level), slice(None))
             merge(acc, ml, where, *softmax_rows(q_ref[pl.ds(low, rows), cols], keys, values, factor))
         share = acc[h] * (1.0 / ml[h][:, 1:2])
@@ -319,22 +379,15 @@
 
 
 def local(tokens, qkv_weight, out_weight, offsets):
-    d = lax.axis_index("dp")
-    ctx = lax.axis_index("ctx")
-    core = ctx & 1
-    odd = (ctx >> 4) & 1
     depth = qkv_weight.shape[0]
-
-    pick = lambda a0, a1, b0, b1: jnp.where(d == 0, jnp.where(core == 0, a0, a1), jnp.where(core == 0, b0, b1))
-    f_src, f_blk = pick(0, 1, 0, 0), pick(2, 0, 1, 0)
-    s_src, s_blk = pick(3, 2, 1 + odd, 0), pick(0, 0, 0, 2)
-    q_src, q_blk = pick(0, 0, 2 - odd, 3), pick(0, 1, 0, 0)
-    f_is_k = pick(1, 1 - odd, 0, 1)
-    zero = jnp.zeros((), jnp.int32)
-    heads = lax.dynamic_slice(offsets, (0, core * HH), (LEVELS, HH)).reshape(-1)
-    meta = jnp.concatenate(
-        [jnp.stack([core, f_src, f_blk, s_src, s_blk, q_src, q_blk, f_is_k, d] + [zero] * 7).astype(jnp.int32), heads]
-    )
+    meta = pl.pallas_call(
+        scalars_kernel,
+        out_shape=jax.ShapeDtypeStruct((META_OFF + LEVELS * HH,), jnp.int32),
+        in_specs=[SCALARS],
+        out_specs=SCALARS,
+        compiler_params=params(1),
+        name="scalars",
+    )(offsets)
 
     x_own = tokens.reshape(TOK, depth)
     first_own = send(payload(first_block, qkv_weight), to_y)
@@ -346,31 +399,34 @@
     relay_fwd = send(relay_own, to_core)
     side_fwd = send(side_own, to_core)
 
+    def along_z(rows):
+        pair = send(rows, to_z1)
+        ring = send(rows, to_z3)
+        return [rows, pair, ring, send(pair, to_z3)]
+
     def gather(block):
         far = send(block[3], to_y2)
-        joined = lax.dynamic_update_slice(block[2], far, (CUT3, 0))
-        pair = send(joined, to_z1)
-        ring = send(joined, to_z3)
-        relay = send(pair, to_z3)
-        return (joined, pair, ring, relay), send(block[1], to_z1)
-
-    first = project(meta, META_FSRC, x_all, qkv_weight, [(first_own, first_fwd)], True)
-    f23, f1_pair = gather(first)
+        joined = join(block[2], far)
+        return along_z(joined), send(block[1], to_z1)
+
+    first = project(meta, META_FSRC, x_all, qkv_weight, [(first_own, first_fwd)], False)
+    f23 = along_z(first[2])
+    f1_pair = send(first[1], to_z1)
+    f3_far = send(collect(f23), to_y2)
     everything = [(first_own, first_fwd), (relay_own, relay_fwd), (side_own, side_fwd)]
     second = project(meta, META_SSRC, x_all, qkv_weight, everything, True)
     s23, s1_pair = gather(second)
     queries = project(meta, META_QSRC, x_all, qkv_weight, everything, False)
 
-    w_own = lax.dynamic_slice(out_weight, (core * WB, zero), (WB, out_weight.shape[1]))
-    rem_own = send(w_own, to_y)
+    rem_own = send(payload(None, out_weight), to_y)
     rem_oth = send(rem_own, to_core)
 
     state = attend(level0_kernel, meta, [queries[0], first[0], second[0]], STATE, ROWS)
     arrays = [queries[1], first[1], f1_pair, second[1], s1_pair, *state]
     state = attend(level1_kernel, meta, arrays, STATE, ROWS >> 1, {6: 0, 7: 1})
-    arrays = [queries[2], *f23, *s23, *state]
+    arrays = [queries[2], *f23, f3_far, *s23, *state]
     outs = [((TOK, WB), jnp.bfloat16)] * 2 + STATE
-    att, att_send, _, _ = attend(level23_kernel, meta, arrays, outs, CUT3, {10: 2, 11: 3})
+    att, att_send, _, _ = attend(level23_kernel, meta, arrays, outs, CUT3, {11: 2, 12: 3})
     att_oth = send(att_send, to_core)
     part = out_project(
         out_own_kernel, meta, [att, out_weight, rem_own], pltpu.VMEM((4, TOK, WB), jnp.float32), HELD, []

time: 156 us -> 136 us (0.87)
  the two profiles are of different devices: /device:TPU:0 before, /device:TPU:15 now
where the time goes in v1:
time: 136 us
  waiting for transfers between devices  54.1 us (40%)
  Pallas kernels  47.8 us (35%)
  starting transfers between devices  32.7 us (24%)
    ppermute x20, waiting for transfers between devices, send(): return lax.ppermute(block, ('dp', 'ctx'), route)  54.1 us
    ppermute x20, starting transfers between devices, send(): return lax.ppermute(block, ('dp', 'ctx'), route)  32.7 us
    pallas_call x3, Pallas kernels, attend(): pl.pallas_call(lambda *refs: kernel(factor, *refs), out_shape=[pltpu.VMEM...  18.6 us
    pallas_call x3, Pallas kernels, project(): pl.pallas_call(lambda *refs: proj_kernel(len(remotes), slot, for_keys, *r...  15.7 us
    pallas_call x2, Pallas kernels, out_project(): pl.pallas_call(kernel, out_shape=out_shape, in_specs=[SCALARS] + [HELD] *...  5.79 us
    pallas_call x3, Pallas kernels, payload(): pl.pallas_call(lambda *refs: payload_kernel(block, *refs), out_shape=pltp...  4.31 us
  transfers between devices with their start and end apart: 20, of which 7 were waited for; matrix products, arithmetic and copies ran while one was open for 0% of the time, Pallas kernels for 32%

profile of v1, /device:TPU:15, one launch (start us, length us, event | category | flops | bytes accessed | tf_op | source)
XLA Modules:
  0.0 136.2 jit_solution(13901498309341015556)
XLA Ops:
  0.0 1.4 %shard_map.46 = bf16[1280,640]{1,0:T(8,128)(2,1)S(1)} custom-call(bf16[2560,1920]{1,0:T(8,128)(2,1)} %refs_2_.5), custom_call_target="tpu_custom_call" | custom-call | tf_op jit(solution)/shard_map/pallas_call | solution.py:166
  1.4 0.0 copy-start.2
  1.5 1.4 %collective-permute-start.1 = (bf16[1280,640]{1,0:T(8,128)(2,1)S(1)}, bf16[1280,640]{1,0:T(8,128)(2,1)S(1)}, u32[]{:S(2)}, u32[]{:S(2)}) collective-permute-start(bf16[1280,640]{1,0:T(8,128)(2,1)S(1)} %shard_map.46), channel_id=1, source_target_pairs={{0,72},{1,65},{2,74},{3,67},{4,76},{5,69},{6,78},{7,71},{64,0},{65... | collective-permute-start | bytes 4915208 | tf_op jit(solution)/shard_map/ppermute | solution.py:35
  2.8 1.4 %shard_map.47 = bf16[1280,640]{1,0:T(8,128)(2,1)S(1)} custom-call(bf16[2560,1920]{1,0:T(8,128)(2,1)} %refs_2_.5), custom_call_target="tpu_custom_call" | custom-call | tf_op jit(solution)/shard_map/pallas_call | solution.py:166
  4.3 1.1 collective-permute-start.5
  5.3 16.4 %collective-permute-done.1.refs_3_ = bf16[1280,640]{1,0:T(8,128)(2,1)S(1)} collective-permute-done((bf16[1280,640]{1,0:T(8,128)(2,1)S(1)}, bf16[1280,640]{1,0:T(8,128)(2,1)S(1)}, u32[]{:S(2)}, u32[]{:S(2)}) %collective-permute-start.1) | collective-permute-done | bytes 1638432 | tf_op jit(solution)/shard_map/ppermute | solution.py:35
  21.8 0.2 collective-permute-start.3
  22.0 0.0 copy-done.2
  22.0 0.0 copy-start.1
  22.0 2.2 %collective-permute-start = (bf16[384,2560]{1,0:T(8,128)(2,1)S(1)}, bf16[384,2560]{1,0:T(8,128)(2,1)S(1)}, u32[]{:S(2)}, u32[]{:S(2)}) collective-permute-start(bf16[384,2560]{1,0:T(8,128)(2,1)S(1)} %bitcast.3), channel_id=1, source_target_pairs={{0,1},{1,0},{2,3},{3,2},{4,5},{5,4},{6,7},{7,6},{64,65},{65,64},{6... | collective-permute-start | bytes 5898248 | tf_op jit(solution)/shard_map/ppermute | solution.py:35
  24.2 0.1 collective-permute-start.2
  24.2 15.1 %collective-permute-done.5.refs_7_ = bf16[1280,640]{1,0:T(8,128)(2,1)S(1)} collective-permute-done((bf16[1280,640]{1,0:T(8,128)(2,1)S(1)}, bf16[1280,640]{1,0:T(8,128)(2,1)S(1)}, u32[]{:S(2)}, u32[]{:S(2)}) %collective-permute-start.5) | collective-permute-done | bytes 1638432 | tf_op jit(solution)/shard_map/ppermute | solution.py:35
  39.3 1.5 %collective-permute-start.6 = (bf16[1280,640]{1,0:T(8,128)(2,1)S(1)}, bf16[1280,640]{1,0:T(8,128)(2,1)S(1)}, u32[]{:S(2)}, u32[]{:S(2)}) collective-permute-start(bf16[1280,640]{1,0:T(8,128)(2,1)S(1)} %collective-permute-done.5.refs_7_), channel_id=1, source_target_pairs={{0,1},{1,0},{2,3},{3,2},{4,5},{5,4},{6,7},{7,6},{64,65},{65,64},{6... | collective-permute-start | bytes 4915208 | tf_op jit(solution)/shard_map/ppermute | solution.py:35
  40.9 1.2 collective-permute-done.3.refs_5_
  42.1 3.6 %collective-permute-start.4 = (bf16[1280,640]{1,0:T(8,128)(2,1)S(1)}, bf16[1280,640]{1,0:T(8,128)(2,1)S(1)}, u32[]{:S(2)}, u32[]{:S(2)}) collective-permute-start(bf16[1280,640]{1,0:T(8,128)(2,1)S(1)} %collective-permute-done.3.refs_5_), channel_id=1, source_target_pairs={{0,1},{1,0},{2,3},{3,2},{4,5},{5,4},{6,7},{7,6},{64,65},{65,64},{6... | collective-permute-start | bytes 4915208 | tf_op jit(solution)/shard_map/ppermute | solution.py:35
  45.7 1.4 %shard_map.56 = bf16[640,1280]{1,0:T(8,128)(2,1)S(1)} custom-call(bf16[1280,1280]{1,0:T(8,128)(2,1)} %w_loc.3), custom_call_target="tpu_custom_call" | custom-call | tf_op jit(solution)/shard_map/pallas_call | solution.py:166
  47.1 1.4 %collective-permute-start.18 = (bf16[640,1280]{1,0:T(8,128)(2,1)S(1)}, bf16[640,1280]{1,0:T(8,128)(2,1)S(1)}, u32[]{:S(2)}, u32[]{:S(2)}) collective-permute-start(bf16[640,1280]{1,0:T(8,128)(2,1)S(1)} %shard_map.56), channel_id=1, source_target_pairs={{0,72},{1,65},{2,74},{3,67},{4,76},{5,69},{6,78},{7,71},{64,0},{65... | collective-permute-start | bytes 4915208 | tf_op jit(solution)/shard_map/ppermute | solution.py:35
  48.5 0.0 copy-done.1
  48.5 1.2 scalars.1.refs_0_.meta
  49.7 0.0 collective-permute-done.x_oth
  49.7 0.0 copy-start.3
  49.7 1.3 copy-done.3
  51.0 2.2 %stage.1.refs_1_ = bf16[768,2560]{1,0:T(8,128)(2,1)S(1)} custom-call(bf16[384,2560]{1,0:T(8,128)(2,1)} %bitcast.2, bf16[384,2560]{1,0:T(8,128)(2,1)} %copy-done.3), custom_call_target="tpu_custom_call" | custom-call | tf_op jit(solution)/shard_map/stage/pallas_call | solution.py:114
  53.1 0.0 collective-permute-done.2.refs_4_
  53.1 5.5 %shard_map.49 = (bf16[768,640]{1,0:T(8,128)(2,1)S(1)}, bf16[384,640]{1,0:T(8,128)(2,1)S(1)}, bf16[288,640]{1,0:T(8,128)(2,1)S(1)}) custom-call(s32[36]{0:T(128)S(1)} %scalars.1.refs_0_.meta, bf16[768,2560]{1,0:T(8,128)(2,1)S(1)} %stage.1.refs_1_, bf16[2560,1920]{1,0:T(8,128)(2,1)} %refs_2_.5, bf16[1280,640]{1,0:T(8,128)(2,1)S(1)} %collective-permute-done.1.refs_3_, ...), custom_call_target="tpu_custom_call" | custom-call | flops 2516582400 | bytes 9175040 | tf_op jit(solution)/shard_map/pallas_call | solution.py:238
  58.6 1.7 %collective-permute-start.7 = (bf16[288,640]{1,0:T(8,128)(2,1)S(1)}, bf16[288,640]{1,0:T(8,128)(2,1)S(1)}, u32[]{:S(2)}, u32[]{:S(2)}) collective-permute-start(bf16[288,640]{1,0:T(8,128)(2,1)S(1)} %get-tuple-element.22.refs_0_.refs_2_), channel_id=1, source_target_pairs={{0,2},{1,3},{2,0},{3,1},{4,6},{5,7},{6,4},{7,5},{64,66},{65,67},{6... | collective-permute-start | bytes 1105928 | tf_op jit(solution)/shard_map/ppermute | solution.py:35
  60.4 0.0 collective-permute-done.6.refs_8_
  60.4 0.0 collective-permute-done.4.refs_6_
  60.4 5.5 %shard_map.51 = (bf16[768,640]{1,0:T(8,128)(2,1)S(1)}, bf16[384,640]{1,0:T(8,128)(2,1)S(1)}, bf16[384,640]{1,0:T(8,128)(2,1)S(1)}, bf16[96,640]{1,0:T(8,128)(2,1)S(1)}) custom-call(s32[36]{0:T(128)S(1)} %scalars.1.refs_0_.meta, bf16[768,2560]{1,0:T(8,128)(2,1)S(1)} %stage.1.refs_1_, bf16[2560,1920]{1,0:T(8,128)(2,1)} %refs_2_.5, ...), custom_call_target="tpu_custom_call" | custom-call | flops 2516582400 | bytes 9175040 | tf_op jit(solution)/shard_map/pallas_call | solution.py:238
  65.9 2.0 %collective-permute-start.11 = (bf16[96,640]{1,0:T(8,128)(2,1)S(1)}, bf16[96,640]{1,0:T(8,128)(2,1)S(1)}, u32[]{:S(2)}, u32[]{:S(2)}) collective-permute-start(bf16[96,640]{1,0:T(8,128)(2,1)S(1)} %get-tuple-element.23), channel_id=1, source_target_pairs={{0,8},{1,9},{2,10},{3,11},{4,12},{5,13},{6,14},{7,15},{64,72},{65,... | collective-permute-start | bytes 368648 | tf_op jit(solution)/shard_map/ppermute | solution.py:35
  67.9 0.0 collective-permute-done.18.rem
  67.9 0.4 collective-permute-start.19
  68.3 1.6 %collective-permute-start.15 = (bf16[384,640]{1,0:T(8,128)(2,1)S(1)}, bf16[384,640]{1,0:T(8,128)(2,1)S(1)}, u32[]{:S(2)}, u32[]{:S(2)}) collective-permute-start(bf16[384,640]{1,0:T(8,128)(2,1)S(1)} %get-tuple-element.26.refs_2_), channel_id=1, source_target_pairs={{0,2},{1,3},{2,0},{3,1},{4,6},{5,7},{6,4},{7,5},{64,66},{65,67},{6... | collective-permute-start | bytes 1474568 | tf_op jit(solution)/shard_map/ppermute | solution.py:35
  69.9 2.0 %collective-permute-done.11.far_rows = bf16[96,640]{1,0:T(8,128)(2,1)S(1)} collective-permute-done((bf16[96,640]{1,0:T(8,128)(2,1)S(1)}, bf16[96,640]{1,0:T(8,128)(2,1)S(1)}, u32[]{:S(2)}, u32[]{:S(2)}) %collective-permute-start.11) | collective-permute-done | bytes 122912 | tf_op jit(solution)/shard_map/ppermute | solution.py:35
  72.0 1.0 collective-permute-start.12
  72.9 2.8 %collective-permute-start.8 = (bf16[288,640]{1,0:T(8,128)(2,1)S(1)}, bf16[288,640]{1,0:T(8,128)(2,1)S(1)}, u32[]{:S(2)}, u32[]{:S(2)}) collective-permute-start(bf16[288,640]{1,0:T(8,128)(2,1)S(1)} %get-tuple-element.22.refs_0_.refs_2_), channel_id=1, source_target_pairs={{0,6},{1,7},{2,4},{3,5},{4,2},{5,3},{6,0},{7,1},{64,70},{65,71},{6... | collective-permute-start | bytes 1105928 | tf_op jit(solution)/shard_map/ppermute | solution.py:35
  75.7 0.0 collective-permute-done.7.refs_1_.refs_3_
  75.7 0.0 collective-permute-start.9
  75.7 7.3 %collective-permute-done.8.refs_2_.refs_4_ = bf16[288,640]{1,0:T(8,128)(2,1)S(1)} collective-permute-done((bf16[288,640]{1,0:T(8,128)(2,1)S(1)}, bf16[288,640]{1,0:T(8,128)(2,1)S(1)}, u32[]{:S(2)}, u32[]{:S(2)}) %collective-permute-start.8) | collective-permute-done | bytes 368672 | tf_op jit(solution)/shard_map/ppermute | solution.py:35
  83.0 0.6 collective-permute-start.16
  83.5 7.3 %collective-permute-done.9.refs_3_.refs_5_ = bf16[288,640]{1,0:T(8,128)(2,1)S(1)} collective-permute-done((bf16[288,640]{1,0:T(8,128)(2,1)S(1)}, bf16[288,640]{1,0:T(8,128)(2,1)S(1)}, u32[]{:S(2)}, u32[]{:S(2)}) %collective-permute-start.9) | collective-permute-done | bytes 368672 | tf_op jit(solution)/shard_map/ppermute | solution.py:35
  90.9 6.2 %collective-permute-start.10 = (bf16[384,640]{1,0:T(8,128)(2,1)S(1)}, bf16[384,640]{1,0:T(8,128)(2,1)S(1)}, u32[]{:S(2)}, u32[]{:S(2)}) collective-permute-start(bf16[384,640]{1,0:T(8,128)(2,1)S(1)} %shard_map.50), channel_id=1, source_target_pairs={{0,8},{1,9},{2,10},{3,11},{4,12},{5,13},{6,14},{7,15},{64,72},{65,... | collective-permute-start | bytes 1474568 | tf_op jit(solution)/shard_map/ppermute | solution.py:35
  97.1 0.0 collective-permute-done.15.refs_3_
  97.1 2.4 %collective-permute-start.13 = (bf16[384,640]{1,0:T(8,128)(2,1)S(1)}, bf16[384,640]{1,0:T(8,128)(2,1)S(1)}, u32[]{:S(2)}, u32[]{:S(2)}) collective-permute-start(bf16[384,640]{1,0:T(8,128)(2,1)S(1)} %shard_map.52.refs_7_), channel_id=1, source_target_pairs={{0,6},{1,7},{2,4},{3,5},{4,2},{5,3},{6,0},{7,1},{64,70},{65,71},{6... | collective-permute-start | bytes 1474568 | tf_op jit(solution)/shard_map/ppermute | solution.py:35
  99.5 0.0 collective-permute-done.12.refs_8_
  99.5 0.3 collective-permute-start.14
  99.8 4.7 %shard_map.48 = (bf16[768,640]{1,0:T(8,128)(2,1)S(1)}, bf16[384,640]{1,0:T(8,128)(2,1)S(1)}, bf16[288,640]{1,0:T(8,128)(2,1)S(1)}) custom-call(s32[36]{0:T(128)S(1)} %scalars.1.refs_0_.meta, bf16[768,2560]{1,0:T(8,128)(2,1)S(1)} %stage.1.refs_1_, bf16[2560,1920]{1,0:T(8,128)(2,1)} %refs_2_.5, bf16[1280,640]{1,0:T(8,128)(2,1)S(1)} %collective-permute-done.1.refs_3_, ...), custom_call_target="tpu_custom_call" | custom-call | flops 2516582400 | bytes 9175040 | tf_op jit(solution)/shard_map/pallas_call | solution.py:238
  104.5 4.8 %shard_map.53 = (f32[5,768,128]{2,1,0:T(8,128)S(1)}, f32[5,768,128]{2,1,0:T(8,128)S(1)}) custom-call(s32[36]{0:T(128)S(1)} %scalars.1.refs_0_.meta, bf16[768,640]{1,0:T(8,128)(2,1)S(1)} %get-tuple-element.28.refs_1_, bf16[768,640]{1,0:T(8,128)(2,1)S(1)} %get-tuple-element.29.refs_2_, bf16[768,640]{1,0:T(8,128)(2,1)S(1)} %get-tuple-element.30.refs_3_), custom_call_target="tpu_custom_call" | custom-call | flops 1509949440 | bytes 2949120 | tf_op jit(solution)/shard_map/pallas_call | solution.py:331
  109.3 0.0 collective-permute-done.16.refs_5_
  109.3 6.1 %shard_map.54 = (f32[5,768,128]{2,1,0:T(8,128)S(1)}, f32[5,768,128]{2,1,0:T(8,128)S(1)}) custom-call(s32[36]{0:T(128)S(1)} %scalars.1.refs_0_.meta, bf16[384,640]{1,0:T(8,128)(2,1)S(1)} %get-tuple-element.25.refs_1_, bf16[384,640]{1,0:T(8,128)(2,1)S(1)} %get-tuple-element.26.refs_2_, ...), custom_call_target="tpu_custom_call", output_to_operand_aliasing={{0}: (6, {}), {1}: (7, {})} | custom-call | flops 754974720 | bytes 2457600 | tf_op jit(solution)/shard_map/pallas_call | solution.py:331
  115.5 0.0 collective-permute-done.10.refs_6_
  115.5 0.0 collective-permute-done.13.refs_9_
  115.5 4.7 %collective-permute-done.14.refs_10_ = bf16[384,640]{1,0:T(8,128)(2,1)S(1)} collective-permute-done((bf16[384,640]{1,0:T(8,128)(2,1)S(1)}, bf16[384,640]{1,0:T(8,128)(2,1)S(1)}, u32[]{:S(2)}, u32[]{:S(2)}) %collective-permute-start.14) | collective-permute-done | bytes 491552 | tf_op jit(solution)/shard_map/ppermute | solution.py:35
  120.2 0.0 copy-start
  120.2 7.6 %shard_map.55 = (bf16[384,640]{1,0:T(8,128)(2,1)S(1)}, bf16[384,640]{1,0:T(8,128)(2,1)S(1)}, f32[5,768,128]{2,1,0:T(8,128)S(1)}, f32[5,768,128]{2,1,0:T(8,128)S(1)}) custom-call(s32[36]{0:T(128)S(1)} %scalars.1.refs_0_.meta, bf16[288,640]{1,0:T(8,128)(2,1)S(1)} %get-tuple-element.21.refs_1_, ...), custom_call_target="tpu_custom_call", output_to_operand_aliasing={{2}: (11, {}), {3}: (12, {})} | custom-call | flops 566231040 | bytes 2334720 | tf_op jit(solution)/shard_map/pallas_call | solution.py:331
  127.8 2.4 %collective-permute-start.17 = (bf16[384,640]{1,0:T(8,128)(2,1)S(1)}, bf16[384,640]{1,0:T(8,128)(2,1)S(1)}, u32[]{:S(2)}, u32[]{:S(2)}) collective-permute-start(bf16[384,640]{1,0:T(8,128)(2,1)S(1)} %get-tuple-element.35), channel_id=1, source_target_pairs={{0,1},{1,0},{2,3},{3,2},{4,5},{5,4},{6,7},{7,6},{64,65},{65,64},{6... | collective-permute-start | bytes 1474568 | tf_op jit(solution)/shard_map/ppermute | solution.py:35
  130.2 0.0 copy-done
  130.2 2.4 %shard_map.57.part = f32[4,384,640]{2,1,0:T(8,128)S(1)} custom-call(s32[36]{0:T(128)S(1)} %scalars.1.refs_0_.meta, bf16[384,640]{1,0:T(8,128)(2,1)S(1)} %get-tuple-element.36.att, bf16[1280,1280]{1,0:T(8,128)(2,1)S(1)} %copy-done, bf16[640,1280]{1,0:T(8,128)(2,1)S(1)} %collective-permute-done.18.rem), custom_call_target="tpu_custom_call" | custom-call | flops 1258291200 | bytes 5242880 | tf_op jit(solution)/shard_map/pallas_call | solution.py:370
  132.6 0.0 collective-permute-done.19.rem
  132.7 0.0 collective-permute-done.17.att
  132.7 3.3 %shard_map.58 = bf16[384,2560]{1,0:T(8,128)(2,1)} custom-call(s32[36]{0:T(128)S(1)} %scalars.1.refs_0_.meta, bf16[384,640]{1,0:T(8,128)(2,1)S(1)} %collective-permute-done.17.att, bf16[1280,1280]{1,0:T(8,128)(2,1)S(1)} %copy-done, bf16[640,1280]{1,0:T(8,128)(2,1)S(1)} %collective-permute-done.19.rem, f32[4,384,640]{2,1,0:T(8,128)S(1)} %shard_map.57.part), custom_call_target="tpu_custom_call" | custom-call | flops 1258291200 | bytes 5242880 | tf_op jit(solution)/shard_map/pallas_call | solution.py:370
  (2 shorter events, 0.0 us)
Async XLA Ops:
  1.4 20.5 %copy-start.2 = (bf16[1,384,2560]{2,1,0:T(8,128)(2,1)S(1)}, bf16[1,384,2560]{2,1,0:T(8,128)(2,1)}, u32[]{:S(2)}) copy-start(bf16[1,384,2560]{2,1,0:T(8,128)(2,1)} %param.4) | copy-start | bytes 5898244
  1.5 20.3 %collective-permute-start.1 = (bf16[1280,640]{1,0:T(8,128)(2,1)S(1)}, bf16[1280,640]{1,0:T(8,128)(2,1)S(1)}, u32[]{:S(2)}, u32[]{:S(2)}) collective-permute-start(bf16[1280,640]{1,0:T(8,128)(2,1)S(1)} %shard_map.46), channel_id=1, source_target_pairs={{0,72},{1,65},{2,74},{3,67},{4,76},{5,69},{6,78},{7,71},{64,0},{65... | collective-permute-start | bytes 4915208 | tf_op jit(solution)/shard_map/ppermute | solution.py:35
  4.3 35.1 %collective-permute-start.5 = (bf16[1280,640]{1,0:T(8,128)(2,1)S(1)}, bf16[1280,640]{1,0:T(8,128)(2,1)S(1)}, u32[]{:S(2)}, u32[]{:S(2)}) collective-permute-start(bf16[1280,640]{1,0:T(8,128)(2,1)S(1)} %shard_map.47), channel_id=1, source_target_pairs={{0,72},{1,65},{2,74},{3,67},{4,76},{5,69},{6,78},{7,71},{64,0},{65... | collective-permute-start | bytes 4915208 | tf_op jit(solution)/shard_map/ppermute | solution.py:35
  21.8 20.3 %collective-permute-start.3 = (bf16[1280,640]{1,0:T(8,128)(2,1)S(1)}, bf16[1280,640]{1,0:T(8,128)(2,1)S(1)}, u32[]{:S(2)}, u32[]{:S(2)}) collective-permute-start(bf16[1280,640]{1,0:T(8,128)(2,1)S(1)} %collective-permute-done.1.refs_3_), channel_id=1, source_target_pairs={{0,48},{1,17},{2,50},{3,19},{4,52},{5,21},{6,54},{7,23},{64,112},{... | collective-permute-start | bytes 4915208 | tf_op jit(solution)/shard_map/ppermute | solution.py:35
  22.0 26.5 %copy-start.1 = (s32[4,10]{1,0:T(4,128)S(1)}, s32[4,10]{1,0:T(4,128)}, u32[]{:S(2)}) copy-start(s32[4,10]{1,0:T(4,128)} %offsets.1) | copy-start | bytes 484
  22.0 27.7 %collective-permute-start = (bf16[384,2560]{1,0:T(8,128)(2,1)S(1)}, bf16[384,2560]{1,0:T(8,128)(2,1)S(1)}, u32[]{:S(2)}, u32[]{:S(2)}) collective-permute-start(bf16[384,2560]{1,0:T(8,128)(2,1)S(1)} %bitcast.3), channel_id=1, source_target_pairs={{0,1},{1,0},{2,3},{3,2},{4,5},{5,4},{6,7},{7,6},{64,65},{65,64},{6... | collective-permute-start | bytes 5898248 | tf_op jit(solution)/shard_map/ppermute | solution.py:35
  24.2 29.0 %collective-permute-start.2 = (bf16[1280,640]{1,0:T(8,128)(2,1)S(1)}, bf16[1280,640]{1,0:T(8,128)(2,1)S(1)}, u32[]{:S(2)}, u32[]{:S(2)}) collective-permute-start(bf16[1280,640]{1,0:T(8,128)(2,1)S(1)} %collective-permute-done.1.refs_3_), channel_id=1, source_target_pairs={{0,1},{1,0},{2,3},{3,2},{4,5},{5,4},{6,7},{7,6},{64,65},{65,64},{6... | collective-permute-start | bytes 4915208 | tf_op jit(solution)/shard_map/ppermute | solution.py:35
  39.3 21.0 %collective-permute-start.6 = (bf16[1280,640]{1,0:T(8,128)(2,1)S(1)}, bf16[1280,640]{1,0:T(8,128)(2,1)S(1)}, u32[]{:S(2)}, u32[]{:S(2)}) collective-permute-start(bf16[1280,640]{1,0:T(8,128)(2,1)S(1)} %collective-permute-done.5.refs_7_), channel_id=1, source_target_pairs={{0,1},{1,0},{2,3},{3,2},{4,5},{5,4},{6,7},{7,6},{64,65},{65,64},{6... | collective-permute-start | bytes 4915208 | tf_op jit(solution)/shard_map/ppermute | solution.py:35
  42.1 18.3 %collective-permute-start.4 = (bf16[1280,640]{1,0:T(8,128)(2,1)S(1)}, bf16[1280,640]{1,0:T(8,128)(2,1)S(1)}, u32[]{:S(2)}, u32[]{:S(2)}) collective-permute-start(bf16[1280,640]{1,0:T(8,128)(2,1)S(1)} %collective-permute-done.3.refs_5_), channel_id=1, source_target_pairs={{0,1},{1,0},{2,3},{3,2},{4,5},{5,4},{6,7},{7,6},{64,65},{65,64},{6... | collective-permute-start | bytes 4915208 | tf_op jit(solution)/shard_map/ppermute | solution.py:35
  47.1 20.8 %collective-permute-start.18 = (bf16[640,1280]{1,0:T(8,128)(2,1)S(1)}, bf16[640,1280]{1,0:T(8,128)(2,1)S(1)}, u32[]{:S(2)}, u32[]{:S(2)}) collective-permute-start(bf16[640,1280]{1,0:T(8,128)(2,1)S(1)} %shard_map.56), channel_id=1, source_target_pairs={{0,72},{1,65},{2,74},{3,67},{4,76},{5,69},{6,78},{7,71},{64,0},{65... | collective-permute-start | bytes 4915208 | tf_op jit(solution)/shard_map/ppermute | solution.py:35
  49.7 1.3 copy-start.3
  58.6 17.1 %collective-permute-start.7 = (bf16[288,640]{1,0:T(8,128)(2,1)S(1)}, bf16[288,640]{1,0:T(8,128)(2,1)S(1)}, u32[]{:S(2)}, u32[]{:S(2)}) collective-permute-start(bf16[288,640]{1,0:T(8,128)(2,1)S(1)} %get-tuple-element.22.refs_0_.refs_2_), channel_id=1, source_target_pairs={{0,2},{1,3},{2,0},{3,1},{4,6},{5,7},{6,4},{7,5},{64,66},{65,67},{6... | collective-permute-start | bytes 1105928 | tf_op jit(solution)/shard_map/ppermute | solution.py:35
  65.9 6.1 %collective-permute-start.11 = (bf16[96,640]{1,0:T(8,128)(2,1)S(1)}, bf16[96,640]{1,0:T(8,128)(2,1)S(1)}, u32[]{:S(2)}, u32[]{:S(2)}) collective-permute-start(bf16[96,640]{1,0:T(8,128)(2,1)S(1)} %get-tuple-element.23), channel_id=1, source_target_pairs={{0,8},{1,9},{2,10},{3,11},{4,12},{5,13},{6,14},{7,15},{64,72},{65,... | collective-permute-start | bytes 368648 | tf_op jit(solution)/shard_map/ppermute | solution.py:35
  67.9 64.7 %collective-permute-start.19 = (bf16[640,1280]{1,0:T(8,128)(2,1)S(1)}, bf16[640,1280]{1,0:T(8,128)(2,1)S(1)}, u32[]{:S(2)}, u32[]{:S(2)}) collective-permute-start(bf16[640,1280]{1,0:T(8,128)(2,1)S(1)} %collective-permute-done.18.rem), channel_id=1, source_target_pairs={{0,1},{1,0},{2,3},{3,2},{4,5},{5,4},{6,7},{7,6},{64,65},{65,64},{6... | collective-permute-start | bytes 4915208 | tf_op jit(solution)/shard_map/ppermute | solution.py:35
  68.3 28.8 %collective-permute-start.15 = (bf16[384,640]{1,0:T(8,128)(2,1)S(1)}, bf16[384,640]{1,0:T(8,128)(2,1)S(1)}, u32[]{:S(2)}, u32[]{:S(2)}) collective-permute-start(bf16[384,640]{1,0:T(8,128)(2,1)S(1)} %get-tuple-element.26.refs_2_), channel_id=1, source_target_pairs={{0,2},{1,3},{2,0},{3,1},{4,6},{5,7},{6,4},{7,5},{64,66},{65,67},{6... | collective-permute-start | bytes 1474568 | tf_op jit(solution)/shard_map/ppermute | solution.py:35
  72.0 27.5 %collective-permute-start.12 = (bf16[384,640]{1,0:T(8,128)(2,1)S(1)}, bf16[384,640]{1,0:T(8,128)(2,1)S(1)}, u32[]{:S(2)}, u32[]{:S(2)}) collective-permute-start(bf16[384,640]{1,0:T(8,128)(2,1)S(1)} %shard_map.52.refs_7_), channel_id=1, source_target_pairs={{0,2},{1,3},{2,0},{3,1},{4,6},{5,7},{6,4},{7,5},{64,66},{65,67},{6... | collective-permute-start | bytes 1474568 | tf_op jit(solution)/shard_map/ppermute | solution.py:35
  72.9 10.1 %collective-permute-start.8 = (bf16[288,640]{1,0:T(8,128)(2,1)S(1)}, bf16[288,640]{1,0:T(8,128)(2,1)S(1)}, u32[]{:S(2)}, u32[]{:S(2)}) collective-permute-start(bf16[288,640]{1,0:T(8,128)(2,1)S(1)} %get-tuple-element.22.refs_0_.refs_2_), channel_id=1, source_target_pairs={{0,6},{1,7},{2,4},{3,5},{4,2},{5,3},{6,0},{7,1},{64,70},{65,71},{6... | collective-permute-start | bytes 1105928 | tf_op jit(solution)/shard_map/ppermute | solution.py:35
  75.7 15.2 %collective-permute-start.9 = (bf16[288,640]{1,0:T(8,128)(2,1)S(1)}, bf16[288,640]{1,0:T(8,128)(2,1)S(1)}, u32[]{:S(2)}, u32[]{:S(2)}) collective-permute-start(bf16[288,640]{1,0:T(8,128)(2,1)S(1)} %collective-permute-done.7.refs_1_.refs_3_), channel_id=1, source_target_pairs={{0,6},{1,7},{2,4},{3,5},{4,2},{5,3},{6,0},{7,1},{64,70},{65,71},{6... | collective-permute-start | bytes 1105928 | tf_op jit(solution)/shard_map/ppermute | solution.py:35
  83.0 26.3 %collective-permute-start.16 = (bf16[384,640]{1,0:T(8,128)(2,1)S(1)}, bf16[384,640]{1,0:T(8,128)(2,1)S(1)}, u32[]{:S(2)}, u32[]{:S(2)}) collective-permute-start(bf16[384,640]{1,0:T(8,128)(2,1)S(1)} %get-tuple-element.27.refs_4_), channel_id=1, source_target_pairs={{0,2},{1,3},{2,0},{3,1},{4,6},{5,7},{6,4},{7,5},{64,66},{65,67},{6... | collective-permute-start | bytes 1474568 | tf_op jit(solution)/shard_map/ppermute | solution.py:35
  90.9 24.5 %collective-permute-start.10 = (bf16[384,640]{1,0:T(8,128)(2,1)S(1)}, bf16[384,640]{1,0:T(8,128)(2,1)S(1)}, u32[]{:S(2)}, u32[]{:S(2)}) collective-permute-start(bf16[384,640]{1,0:T(8,128)(2,1)S(1)} %shard_map.50), channel_id=1, source_target_pairs={{0,8},{1,9},{2,10},{3,11},{4,12},{5,13},{6,14},{7,15},{64,72},{65,... | collective-permute-start | bytes 1474568 | tf_op jit(solution)/shard_map/ppermute | solution.py:35
  97.1 18.4 %collective-permute-start.13 = (bf16[384,640]{1,0:T(8,128)(2,1)S(1)}, bf16[384,640]{1,0:T(8,128)(2,1)S(1)}, u32[]{:S(2)}, u32[]{:S(2)}) collective-permute-start(bf16[384,640]{1,0:T(8,128)(2,1)S(1)} %shard_map.52.refs_7_), channel_id=1, source_target_pairs={{0,6},{1,7},{2,4},{3,5},{4,2},{5,3},{6,0},{7,1},{64,70},{65,71},{6... | collective-permute-start | bytes 1474568 | tf_op jit(solution)/shard_map/ppermute | solution.py:35
  99.5 20.7 %collective-permute-start.14 = (bf16[384,640]{1,0:T(8,128)(2,1)S(1)}, bf16[384,640]{1,0:T(8,128)(2,1)S(1)}, u32[]{:S(2)}, u32[]{:S(2)}) collective-permute-start(bf16[384,640]{1,0:T(8,128)(2,1)S(1)} %collective-permute-done.12.refs_8_), channel_id=1, source_target_pairs={{0,6},{1,7},{2,4},{3,5},{4,2},{5,3},{6,0},{7,1},{64,70},{65,71},{6... | collective-permute-start | bytes 1474568 | tf_op jit(solution)/shard_map/ppermute | solution.py:35
  120.2 10.0 %copy-start = (bf16[1280,1280]{1,0:T(8,128)(2,1)S(1)}, bf16[1280,1280]{1,0:T(8,128)(2,1)}, u32[]{:S(2)}) copy-start(bf16[1280,1280]{1,0:T(8,128)(2,1)} %w_loc.3) | copy-start | bytes 9830404
  127.8 4.8 %collective-permute-start.17 = (bf16[384,640]{1,0:T(8,128)(2,1)S(1)}, bf16[384,640]{1,0:T(8,128)(2,1)S(1)}, u32[]{:S(2)}, u32[]{:S(2)}) collective-permute-start(bf16[384,640]{1,0:T(8,128)(2,1)S(1)} %get-tuple-element.35), channel_id=1, source_target_pairs={{0,1},{1,0},{2,3},{3,2},{4,5},{5,4},{6,7},{7,6},{64,65},{65,64},{6... | collective-permute-start | bytes 1474568 | tf_op jit(solution)/shard_map/ppermute | solution.py:35

commit v2 on v1

--- a/solution.py
+++ b/solution.py
@@ -12,7 +12,6 @@
 HH = 5
 WB = HH * HD
 LEVELS = 4
-KC = 1280
 LOG2E = 1.4426950408889634
 
 META_CORE, META_FSRC, META_FBLK, META_SSRC, META_SBLK, META_QSRC, META_QBLK, META_FK, META_DP = range(9)
@@ -152,20 +151,20 @@
     )(*held(*blocks))
 
 
-def payload_kernel(block, w, out, sem):
+def payload_kernel(block, part, parts, w, out, sem):
     core = lax.rem(lax.axis_index("ctx"), 2)
-    half = w.shape[0] // 2
-    rows = pl.ds(pl.multiple_of(core * half, half), half)
+    size = w.shape[0] // 2 // parts
+    rows = pl.ds(pl.multiple_of((core * parts + part) * size, size), size)
     source = w.at[rows] if block is None else w.at[rows, pl.ds(pl.multiple_of(block() * WB, HD), WB)]
     copy = pltpu.make_async_copy(source, out, sem.at[0])
     copy.start()
     copy.wait()
 
 
-def payload(block, w):
-    return pl.pallas_call(
-        lambda *refs: payload_kernel(block, *refs),
-        out_shape=pltpu.VMEM((w.shape[0] // 2, w.shape[1] if block is None else WB), w.dtype),
+def payload(block, w, part=0, parts=1):
+    return pl.pallas_call(
+        lambda *refs: payload_kernel(block, part, parts, *refs),
+        out_shape=pltpu.VMEM((w.shape[0] // 2 // parts, w.shape[1] if block is None else WB), w.dtype),
         in_specs=[FAR],
         out_specs=HELD,
         scratch_shapes=[pltpu.SemaphoreType.DMA((1,))],
@@ -181,42 +180,51 @@
 CUT2, CUT3 = ROWS >> 2, (ROWS >> 2) + (ROWS >> 3)
 
 
-def proj_kernel(remote, slot, for_keys, meta, x_all, w_loc, *rest):
-    halves = rest[: 2 * remote]
-    outs, (wbuf, acc, wsem) = rest[2 * remote : -3], rest[-3:]
-    chunks = w_loc.shape[0] // KC
+def proj_kernel(counts, slot, phases, for_keys, meta, x_all, w_loc, *rest):
+    ins, rest = list(rest[: sum(counts)]), rest[sum(counts) :]
+    remotes = [[ins.pop(0) for _ in range(n)] for n in counts]
+    acc_in = None
+    if 0 not in phases:
+        acc_in, rest = rest[0], rest[1:]
+    outs, (wbuf, wsem) = rest[:-2], rest[-2:]
+    if 1 in phases:
+        acc, outs = outs[-1], outs[:-1]
+    else:
+        acc = outs[0]
+    half = w_loc.shape[0] // 2
     core = meta[META_CORE]
     src = meta[slot]
     col = pl.multiple_of(meta[slot + 1] * WB, HD)
-    for i in range(chunks):
-        rows = pl.ds(i * KC, KC)
+    base = [pl.multiple_of((core if p == 0 else 1 - core) * half, half) for p in range(2)]
+    for i, p in enumerate(phases):
 
         @pl.when(src == 0)
         def _():
-            pltpu.make_async_copy(w_loc.at[rows, pl.ds(col, WB)], wbuf.at[rows], wsem.at[i]).start()
-
-        part = i * 2 // chunks
-        low = pl.ds((i - part * (chunks // 2)) * KC, KC)
-        for r in range(remote):
-            for own in range(2):
-
-                @pl.when((src == r + 1) & ((core == part) if own else (core != part)))
-                def _():
-                    pltpu.make_async_copy(halves[2 * r + 1 - own].at[low], wbuf.at[rows], wsem.at[i]).start()
-
-    for i in range(chunks):
-        rows = pl.ds(i * KC, KC)
-        pltpu.make_async_copy(w_loc.at[rows, pl.ds(0, WB)], wbuf.at[rows], wsem.at[i]).wait()
+            pltpu.make_async_copy(w_loc.at[pl.ds(base[p], half), pl.ds(col, WB)], wbuf.at[i], wsem.at[i]).start()
+
+        for r in range(len(remotes) // len(phases)):
+            parts = remotes[r * len(phases) + i]
+
+            @pl.when(src == r + 1)
+            def _():
+                size = half // len(parts)
+                for n, part in enumerate(parts):
+                    pltpu.make_async_copy(part, wbuf.at[i, pl.ds(n * size, size)], wsem.at[i]).start()
+
+    for i, p in enumerate(phases):
+        pltpu.make_async_copy(w_loc.at[pl.ds(0, half), pl.ds(0, WB)], wbuf.at[i], wsem.at[i]).wait()
         for g in range(2):
             span = pl.ds(g * TOK, TOK)
-            got = jnp.dot(x_all[span, rows], wbuf[rows], preferred_element_type=jnp.float32)
+            got = jnp.dot(x_all[span, pl.ds(base[p], half)], wbuf[i], preferred_element_type=jnp.float32)
             for h in range(HH):
                 piece = got[:, h * HD : (h + 1) * HD]
-                if i > 0:
-                    piece = acc[h, span] + piece
+                if p == 1:
+                    piece = (acc if acc_in is None else acc_in)[h, span] + piece
                 acc[h, span] = piece
-                if i == chunks - 1:
+                if p == 1:
                     outs[0][span, pl.ds(h * HD, HD)] = piece.astype(jnp.bfloat16)
+    if 1 not in phases:
+        return
     for h in range(HH):
         cols = pl.ds(h * HD, HD)
         kept = [
@@ -231,25 +239,30 @@
             outs[3][:, cols] = kept[2]
 
 
-def project(meta, slot, x_all, w_loc, remotes, for_keys):
+def project(meta, slot, x_all, w_loc, remotes, for_keys=False, phases=(0, 1), acc=None):
     depth = w_loc.shape[0]
-    flat = [half for pair in remotes for half in pair]
-    shapes = [(ROWS, WB), (ROWS >> 1, WB)] + ([(ROWS >> 1, WB), (ROWS >> 3, WB)] if for_keys else [(CUT3, WB)])
-    return pl.pallas_call(
-        lambda *refs: proj_kernel(len(remotes), slot, for_keys, *refs),
-        out_shape=[pltpu.VMEM(s, jnp.bfloat16) for s in shapes],
-        in_specs=[SCALARS, HELD, FAR] + [HELD] * len(flat),
+    groups = [pair[p] for pair in remotes for p in phases]
+    flat = [part for group in groups for part in group]
+    acc_shape = ((HH, ROWS, HD), jnp.float32)
+    if phases == (0,):
+        shapes = [acc_shape]
+    else:
+        shapes = [(ROWS, WB), (ROWS >> 1, WB)] + ([(ROWS >> 1, WB), (ROWS >> 3, WB)] if for_keys else [(CUT3, WB)])
+        shapes = [(n, jnp.bfloat16) for n in shapes]
+    scratch = [pltpu.VMEM(*acc_shape)] if 1 in phases else []
+    scratch += [pltpu.VMEM((len(phases), depth // 2, WB), jnp.bfloat16), pltpu.SemaphoreType.DMA((len(phases),))]
+    more = [] if acc is None else [acc]
+    return pl.pallas_call(
+        lambda *refs: proj_kernel([len(g) for g in groups], slot, phases, for_keys, *refs),
+        out_shape=[pltpu.VMEM(*n) for n in shapes],
+        in_specs=[SCALARS, HELD, FAR] + [HELD] * (len(flat) + len(more)),
         out_specs=[HELD] * len(shapes),
-        scratch_shapes=[
-            pltpu.VMEM((depth, WB), jnp.bfloat16),
-            pltpu.VMEM((HH, ROWS, HD), jnp.float32),
-            pltpu.SemaphoreType.DMA((depth // KC,)),
-        ],
+        scratch_shapes=scratch,
         compiler_params=params(16),
         cost_estimate=pl.CostEstimate(
-            flops=2 * ROWS * depth * WB, transcendentals=0, bytes_accessed=2 * (ROWS * depth + depth * WB + 2 * ROWS * WB)
+            flops=ROWS * depth * WB * len(phases), transcendentals=0, bytes_accessed=2 * (ROWS * depth + depth * WB + 2 * ROWS * WB)
         ),
-    )(meta, *held(x_all), *far(w_loc), *held(*flat))
+    )(meta, *held(x_all), *far(w_loc), *held(*flat, *more))
 
 
 def softmax_rows(q, keys, values, factor):
@@ -265,18 +278,19 @@
     return blend, top * factor, total
 
 
-def pack(top, total):
-    lane = lax.broadcasted_iota(jnp.int32, (1, HD), 1)
-    return jnp.where(lane == 0, top, total)
-
-
-def merge(acc_ref, ml_ref, where, blend, top, total):
-    old = ml_ref[where]
-    old_top, old_total = old[:, 0:1], old[:, 1:2]
-    newest = jnp.maximum(old_top, top)
-    former, fresh = jnp.exp2(old_top - newest), jnp.exp2(top - newest)
+def lanes(column):
+    return jnp.broadcast_to(column, (column.shape[0], HD))
+
+
+def merge(state, where, blend, top, total):
+    acc_ref, top_ref, total_ref = state
+    old = top_ref[where]
+    top = lanes(top)
+    newest = jnp.maximum(old, top)
+    former, fresh = jnp.exp2(old - newest), jnp.exp2(top - newest)
     acc_ref[where] = acc_ref[where] * former + blend * fresh
-    ml_ref[where] = pack(newest, old_total * former + total * fresh)
+    total_ref[where] = total_ref[where] * former + lanes(total) * fresh
+    top_ref[where] = newest
 
 
 def choose(meta, firsts, seconds):
@@ -286,26 +300,27 @@
     return [jnp.where(f_is_k, f, s)], [jnp.where(f_is_k, s, f)]
 
 
-def level0_kernel(factor, meta, q_ref, f_ref, s_ref, acc_ref, ml_ref):
+def level0_kernel(factor, meta, q_ref, f_ref, s_ref, acc_ref, top_ref, total_ref):
     for h in range(HH):
         cols = pl.ds(h * HD, HD)
         keys, values = choose(meta, [f_ref[:, cols]], [s_ref[:, cols]])
         for start in range(0, ROWS, TOK):
             blend, top, total = softmax_rows(q_ref[pl.ds(start, TOK), cols], keys, values, factor)
             acc_ref[h, pl.ds(start, TOK), :] = blend
-            ml_ref[h, pl.ds(start, TOK), :] = pack(top, total)
-
-
-def level1_kernel(factor, meta, q_ref, f0, f1, s0, s1, _acc, _ml, acc_ref, ml_ref):
+            top_ref[h, pl.ds(start, TOK), :] = lanes(top)
+            total_ref[h, pl.ds(start, TOK), :] = lanes(total)
+
+
+def level1_kernel(factor, meta, q_ref, f0, f1, s0, s1, *refs):
     for h in range(HH):
         cols = pl.ds(h * HD, HD)
         keys, values = choose(meta, [f0[:, cols], f1[:, cols]], [s0[:, cols], s1[:, cols]])
         where = (h, pl.ds(meta[META_OFF + HH + h], TOK, stride=2), slice(None))
-        merge(acc_ref, ml_ref, where, *softmax_rows(q_ref[:, cols], keys, values, factor))
+        merge(refs[3:], where, *softmax_rows(q_ref[:, cols], keys, values, factor))
 
 
 def level23_kernel(factor, meta, q_ref, *refs):
-    fs, f_far, ss, (own_ref, oth_ref, acc, ml) = refs[:4], refs[4], refs[5:9], refs[11:]
+    fs, f_far, ss, (own_ref, oth_ref, *state) = refs[:4], refs[4], refs[5:9], refs[12:]
     third = ROWS >> 3
     for h in range(HH):
         cols = pl.ds(h * HD, HD)
@@ -317,13 +332,13 @@
                 seconds = [s[CUT2:, cols] for s in ss]
             keys, values = choose(meta, firsts, seconds)
             where = (h, pl.ds(meta[META_OFF + level * HH + h], rows, stride=1 << level), slice(None))
-            merge(acc, ml, where, *softmax_rows(q_ref[pl.ds(low, rows), cols], keys, values, factor))
-        share = acc[h] * (1.0 / ml[h][:, 1:2])
+            merge(state, where, *softmax_rows(q_ref[pl.ds(low, rows), cols], keys, values, factor))
+        share = state[0][h] * (1.0 / state[2][h])
         own_ref[:, cols] = share[:TOK].astype(jnp.bfloat16)
         oth_ref[:, cols] = share[TOK:].astype(jnp.bfloat16)
 
 
-STATE = [((HH, ROWS, HD), jnp.float32)] * 2
+STATE = [((HH, ROWS, HD), jnp.float32)] * 3
 
 
 def attend(kernel, meta, arrays, outs, rows, alias=None):
@@ -390,43 +405,43 @@
     )(offsets)
 
     x_own = tokens.reshape(TOK, depth)
-    first_own = send(payload(first_block, qkv_weight), to_y)
+    parts = range(2)
+    first_own = [send(payload(first_block, qkv_weight, n, 2), to_y) for n in parts]
     x_oth = send(x_own, to_core)
-    side_own = send(payload(lambda: 1, qkv_weight), to_y)
+    side_own = [send(payload(lambda: 1, qkv_weight), to_y)]
     x_all = stage(x_own, x_oth)
-    first_fwd = send(first_own, to_core)
-    relay_own = send(first_own, to_x)
-    relay_fwd = send(relay_own, to_core)
-    side_fwd = send(side_own, to_core)
+    first_fwd = [send(first_own[n], to_core) for n in parts]
+    relay_own = [send(first_own[n], to_x) for n in parts]
+    relay_fwd = [send(relay_own[n], to_core) for n in parts]
+    side_fwd = [send(side_own[0], to_core)]
 
     def along_z(rows):
         pair = send(rows, to_z1)
         ring = send(rows, to_z3)
         return [rows, pair, ring, send(pair, to_z3)]
 
-    def gather(block):
-        far = send(block[3], to_y2)
-        joined = join(block[2], far)
-        return along_z(joined), send(block[1], to_z1)
-
-    first = project(meta, META_FSRC, x_all, qkv_weight, [(first_own, first_fwd)], False)
+    first = project(meta, META_FSRC, x_all, qkv_weight, [(first_own, first_fwd)])
     f23 = along_z(first[2])
     f1_pair = send(first[1], to_z1)
     f3_far = send(collect(f23), to_y2)
+
     everything = [(first_own, first_fwd), (relay_own, relay_fwd), (side_own, side_fwd)]
-    second = project(meta, META_SSRC, x_all, qkv_weight, everything, True)
-    s23, s1_pair = gather(second)
-    queries = project(meta, META_QSRC, x_all, qkv_weight, everything, False)
+    (acc,) = project(meta, META_SSRC, x_all, qkv_weight, everything, phases=(0,))
+    second = project(meta, META_SSRC, x_all, qkv_weight, everything, True, phases=(1,), acc=acc)
+    s_far = send(second[3], to_y2)
+    s23 = along_z(join(second[2], s_far))
+    s1_pair = send(second[1], to_z1)
+    queries = project(meta, META_QSRC, x_all, qkv_weight, everything)
 
     rem_own = send(payload(None, out_weight), to_y)
     rem_oth = send(rem_own, to_core)
 
     state = attend(level0_kernel, meta, [queries[0], first[0], second[0]], STATE, ROWS)
     arrays = [queries[1], first[1], f1_pair, second[1], s1_pair, *state]
-    state = attend(level1_kernel, meta, arrays, STATE, ROWS >> 1, {6: 0, 7: 1})
+    state = attend(level1_kernel, meta, arrays, STATE, ROWS >> 1, {6: 0, 7: 1, 8: 2})
     arrays = [queries[2], *f23, f3_far, *s23, *state]
     outs = [((TOK, WB), jnp.bfloat16)] * 2 + STATE
-    att, att_send, _, _ = attend(level23_kernel, meta, arrays, outs, CUT3, {11: 2, 12: 3})
+    att, att_send, *_ = attend(level23_kernel, meta, arrays, outs, CUT3, {11: 2, 12: 3, 13: 4})
     att_oth = send(att_send, to_core)
     part = out_project(
         out_own_kernel, meta, [att, out_weight, rem_own], pltpu.VMEM((4, TOK, WB), jnp.float32), HELD, []

time: 136 us -> 139 us (1.022)
  waiting for transfers between devices: 54.1 us -> 64 us
  starting transfers between devices: 32.7 us -> 29.1 us
  Pallas kernels: 47.8 us -> 45.1 us
    ppermute x20 -> x24, waiting for transfers between devices: 54.1 us -> 64 us  [send(): return lax.ppermute(block, ('dp', 'ctx'), route)]
    pallas_call x3, Pallas kernels: 18.6 us -> 13 us  [attend(): pl.pallas_call(lambda *refs: kernel(factor, *refs), out_shape=[pltpu.VMEM...]
    ppermute x20 -> x24, starting transfers between devices: 32.7 us -> 29.1 us  [send(): return lax.ppermute(block, ('dp', 'ctx'), route)]
    pallas_call x6 -> x8, Pallas kernels: 20 us -> 23 us  [the longest x4 17.8 us: project(): pl.pallas_call(lambda *refs: proj_kernel([len(g) for g in groups], slot,...]
  transfers between devices with their start and end apart: 20 -> 24, of which waited for: 7 -> 7; matrix products, arithmetic and copies ran while one was open for 0% -> 0% of each run, Pallas kernels for 32% -> 29%
where the time goes in v2:
time: 139 us
  waiting for transfers between devices  64 us (46%)
  Pallas kernels  45.1 us (32%)
  starting transfers between devices  29.1 us (21%)
    ppermute x24, waiting for transfers between devices, send(): return lax.ppermute(block, ('dp', 'ctx'), route)  64 us
    ppermute x24, starting transfers between devices, send(): return lax.ppermute(block, ('dp', 'ctx'), route)  29.1 us
    pallas_call x4, Pallas kernels, project(): pl.pallas_call(lambda *refs: proj_kernel([len(g) for g in groups], slot,...  17.8 us
    pallas_call x3, Pallas kernels, attend(): pl.pallas_call(lambda *refs: kernel(factor, *refs), out_shape=[pltpu.VMEM...  13 us
    pallas_call x2, Pallas kernels, out_project(): pl.pallas_call(kernel, out_shape=out_shape, in_specs=[SCALARS] + [HELD] *...  5.79 us
    pallas_call x4, Pallas kernels, payload(): pl.pallas_call(lambda *refs: payload_kernel(block, part, parts, *refs), o...  5.18 us
  transfers between devices with their start and end apart: 24, of which 7 were waited for; matrix products, arithmetic and copies ran while one was open for 0% of the time, Pallas kernels for 29%

profile of v2, /device:TPU:15, one launch (start us, length us, event | category | flops | bytes accessed | tf_op | source)
XLA Modules:
  0.0 138.7 jit_solution(17505801748806642738)
XLA Ops:
  0.0 1.4 %shard_map.48 = bf16[1280,640]{1,0:T(8,128)(2,1)S(1)} custom-call(bf16[2560,1920]{1,0:T(8,128)(2,1)} %refs_2_.7), custom_call_target="tpu_custom_call" | custom-call | tf_op jit(solution)/shard_map/pallas_call | solution.py:165
  1.4 1.4 collective-permute-start.9
  2.8 1.2 shard_map.46
  4.0 0.0 copy-start.2
  4.0 1.1 collective-permute-start.1
  5.1 1.2 shard_map.47
  6.2 0.2 collective-permute-start.2
  6.4 2.4 %collective-permute-start = (bf16[384,2560]{1,0:T(8,128)(2,1)S(1)}, bf16[384,2560]{1,0:T(8,128)(2,1)S(1)}, u32[]{:S(2)}, u32[]{:S(2)}) collective-permute-start(bf16[384,2560]{1,0:T(8,128)(2,1)S(1)} %bitcast.3), channel_id=1, source_target_pairs={{0,1},{1,0},{2,3},{3,2},{4,5},{5,4},{6,7},{7,6},{64,65},{65,64},{6... | collective-permute-start | bytes 5898248 | tf_op jit(solution)/shard_map/ppermute | solution.py:34
  8.9 21.7 %collective-permute-done.1.refs_3_ = bf16[640,640]{1,0:T(8,128)(2,1)S(1)} collective-permute-done((bf16[640,640]{1,0:T(8,128)(2,1)S(1)}, bf16[640,640]{1,0:T(8,128)(2,1)S(1)}, u32[]{:S(2)}, u32[]{:S(2)}) %collective-permute-start.1) | collective-permute-done | bytes 819232 | tf_op jit(solution)/shard_map/ppermute | solution.py:34
  30.6 0.2 collective-permute-start.5
  30.8 8.6 %collective-permute-done.2.refs_4_ = bf16[640,640]{1,0:T(8,128)(2,1)S(1)} collective-permute-done((bf16[640,640]{1,0:T(8,128)(2,1)S(1)}, bf16[640,640]{1,0:T(8,128)(2,1)S(1)}, u32[]{:S(2)}, u32[]{:S(2)}) %collective-permute-start.2) | collective-permute-done | bytes 819232 | tf_op jit(solution)/shard_map/ppermute | solution.py:34
  39.3 0.2 collective-permute-start.6
  39.5 2.2 %collective-permute-start.3 = (bf16[640,640]{1,0:T(8,128)(2,1)S(1)}, bf16[640,640]{1,0:T(8,128)(2,1)S(1)}, u32[]{:S(2)}, u32[]{:S(2)}) collective-permute-start(bf16[640,640]{1,0:T(8,128)(2,1)S(1)} %collective-permute-done.1.refs_3_), channel_id=1, source_target_pairs={{0,1},{1,0},{2,3},{3,2},{4,5},{5,4},{6,7},{7,6},{64,65},{65,64},{6... | collective-permute-start | bytes 2457608 | tf_op jit(solution)/shard_map/ppermute | solution.py:34
  41.7 0.0 collective-permute-done.9.refs_11_.refs_7_
  41.7 0.0 collective-permute-start.10
  41.7 1.4 %shard_map.58 = bf16[640,1280]{1,0:T(8,128)(2,1)S(1)} custom-call(bf16[1280,1280]{1,0:T(8,128)(2,1)} %w_loc.3), custom_call_target="tpu_custom_call" | custom-call | tf_op jit(solution)/shard_map/pallas_call | solution.py:165
  43.1 0.0 collective-permute-done.5.refs_7_.refs_5_
  43.2 1.4 collective-permute-start.22
  44.5 6.3 %collective-permute-done.6.refs_8_.refs_6_ = bf16[640,640]{1,0:T(8,128)(2,1)S(1)} collective-permute-done((bf16[640,640]{1,0:T(8,128)(2,1)S(1)}, bf16[640,640]{1,0:T(8,128)(2,1)S(1)}, u32[]{:S(2)}, u32[]{:S(2)}) %collective-permute-start.6) | collective-permute-done | bytes 819232 | tf_op jit(solution)/shard_map/ppermute | solution.py:34
  50.8 3.6 %collective-permute-start.4 = (bf16[640,640]{1,0:T(8,128)(2,1)S(1)}, bf16[640,640]{1,0:T(8,128)(2,1)S(1)}, u32[]{:S(2)}, u32[]{:S(2)}) collective-permute-start(bf16[640,640]{1,0:T(8,128)(2,1)S(1)} %collective-permute-done.2.refs_4_), channel_id=1, source_target_pairs={{0,1},{1,0},{2,3},{3,2},{4,5},{5,4},{6,7},{7,6},{64,65},{65,64},{6... | collective-permute-start | bytes 2457608 | tf_op jit(solution)/shard_map/ppermute | solution.py:34
  54.4 0.0 collective-permute-done.3.refs_5_.refs_3_
  54.4 0.0 collective-permute-start.7
  54.4 0.0 collective-permute-done.x_oth
  54.4 0.0 copy-start.3
  54.4 0.5 collective-permute-start.8
  54.9 1.2 scalars.1.refs_0_.meta
  56.2 2.2 %stage.1.refs_1_ = bf16[768,2560]{1,0:T(8,128)(2,1)S(1)} custom-call(bf16[384,2560]{1,0:T(8,128)(2,1)} %bitcast.2, bf16[384,2560]{1,0:T(8,128)(2,1)} %copy-done.3), custom_call_target="tpu_custom_call" | custom-call | tf_op jit(solution)/shard_map/stage/pallas_call | solution.py:113
  58.3 0.0 collective-permute-done.4.refs_6_.refs_4_
  58.3 5.5 %shard_map.50 = (bf16[768,640]{1,0:T(8,128)(2,1)S(1)}, bf16[384,640]{1,0:T(8,128)(2,1)S(1)}, bf16[288,640]{1,0:T(8,128)(2,1)S(1)}) custom-call(s32[36]{0:T(128)S(1)} %scalars.1.refs_0_.meta, bf16[768,2560]{1,0:T(8,128)(2,1)S(1)} %stage.1.refs_1_, bf16[2560,1920]{1,0:T(8,128)(2,1)} %refs_2_.7, bf16[640,640]{1,0:T(8,128)(2,1)S(1)} %collective-permute-done.1.refs_3_, ...), custom_call_target="tpu_custom_call" | custom-call | flops 2516582400 | bytes 9175040 | tf_op jit(solution)/shard_map/pallas_call | solution.py:255
  63.8 1.7 %collective-permute-start.11 = (bf16[288,640]{1,0:T(8,128)(2,1)S(1)}, bf16[288,640]{1,0:T(8,128)(2,1)S(1)}, u32[]{:S(2)}, u32[]{:S(2)}) collective-permute-start(bf16[288,640]{1,0:T(8,128)(2,1)S(1)} %get-tuple-element.24.refs_0_.refs_2_), channel_id=1, source_target_pairs={{0,2},{1,3},{2,0},{3,1},{4,6},{5,7},{6,4},{7,5},{64,66},{65,67},{6... | collective-permute-start | bytes 1105928 | tf_op jit(solution)/shard_map/ppermute | solution.py:34
  65.6 3.7 %shard_map.52.refs_8_ = f32[5,768,128]{2,1,0:T(8,128)S(1)} custom-call(s32[36]{0:T(128)S(1)} %scalars.1.refs_0_.meta, bf16[768,2560]{1,0:T(8,128)(2,1)S(1)} %stage.1.refs_1_, bf16[2560,1920]{1,0:T(8,128)(2,1)} %refs_2_.7, bf16[640,640]{1,0:T(8,128)(2,1)S(1)} %collective-permute-done.1.refs_3_, bf16[640,640]{1,0:T(8,128)(2,1)S(1)} %collective-permute-done.2.refs_4_, ...), custom_call_target="tpu_custom_call" | custom-call | flops 1258291200 | bytes 9175040 | tf_op jit(solution)/shard_map/pallas_call | solution.py:255
  69.2 0.0 collective-permute-done.7.refs_9_.refs_5_
  69.2 0.0 collective-permute-done.8.refs_10_.refs_6_
  69.3 0.0 collective-permute-done.10.refs_12_.refs_7_
  69.3 4.0 %shard_map.53 = (bf16[768,640]{1,0:T(8,128)(2,1)S(1)}, bf16[384,640]{1,0:T(8,128)(2,1)S(1)}, bf16[384,640]{1,0:T(8,128)(2,1)S(1)}, bf16[96,640]{1,0:T(8,128)(2,1)S(1)}) custom-call(s32[36]{0:T(128)S(1)} %scalars.1.refs_0_.meta, bf16[768,2560]{1,0:T(8,128)(2,1)S(1)} %stage.1.refs_1_, bf16[2560,1920]{1,0:T(8,128)(2,1)} %refs_2_.7, ...), custom_call_target="tpu_custom_call" | custom-call | flops 1258291200 | bytes 9175040 | tf_op jit(solution)/shard_map/pallas_call | solution.py:255
  73.2 3.3 %collective-permute-start.15 = (bf16[96,640]{1,0:T(8,128)(2,1)S(1)}, bf16[96,640]{1,0:T(8,128)(2,1)S(1)}, u32[]{:S(2)}, u32[]{:S(2)}) collective-permute-start(bf16[96,640]{1,0:T(8,128)(2,1)S(1)} %get-tuple-element.25), channel_id=1, source_target_pairs={{0,8},{1,9},{2,10},{3,11},{4,12},{5,13},{6,14},{7,15},{64,72},{65,... | collective-permute-start | bytes 368648 | tf_op jit(solution)/shard_map/ppermute | solution.py:34
  76.6 0.0 collective-permute-done.22.rem
  76.6 0.0 collective-permute-start.23
  76.6 0.0 collective-permute-start.19
  76.6 2.2 %collective-permute-done.15.far_rows = bf16[96,640]{1,0:T(8,128)(2,1)S(1)} collective-permute-done((bf16[96,640]{1,0:T(8,128)(2,1)S(1)}, bf16[96,640]{1,0:T(8,128)(2,1)S(1)}, u32[]{:S(2)}, u32[]{:S(2)}) %collective-permute-start.15) | collective-permute-done | bytes 122912 | tf_op jit(solution)/shard_map/ppermute | solution.py:34
  78.8 0.1 collective-permute-start.16
  78.9 3.6 %collective-permute-start.12 = (bf16[288,640]{1,0:T(8,128)(2,1)S(1)}, bf16[288,640]{1,0:T(8,128)(2,1)S(1)}, u32[]{:S(2)}, u32[]{:S(2)}) collective-permute-start(bf16[288,640]{1,0:T(8,128)(2,1)S(1)} %get-tuple-element.24.refs_0_.refs_2_), channel_id=1, source_target_pairs={{0,6},{1,7},{2,4},{3,5},{4,2},{5,3},{6,0},{7,1},{64,70},{65,71},{6... | collective-permute-start | bytes 1105928 | tf_op jit(solution)/shard_map/ppermute | solution.py:34
  82.5 0.0 collective-permute-done.11.refs_1_.refs_3_
  82.5 0.0 collective-permute-start.13
  82.5 9.1 %collective-permute-done.12.refs_2_.refs_4_ = bf16[288,640]{1,0:T(8,128)(2,1)S(1)} collective-permute-done((bf16[288,640]{1,0:T(8,128)(2,1)S(1)}, bf16[288,640]{1,0:T(8,128)(2,1)S(1)}, u32[]{:S(2)}, u32[]{:S(2)}) %collective-permute-start.12) | collective-permute-done | bytes 368672 | tf_op jit(solution)/shard_map/ppermute | solution.py:34
  91.7 0.0 collective-permute-start.20
  91.7 7.5 %collective-permute-done.13.refs_3_.refs_5_ = bf16[288,640]{1,0:T(8,128)(2,1)S(1)} collective-permute-done((bf16[288,640]{1,0:T(8,128)(2,1)S(1)}, bf16[288,640]{1,0:T(8,128)(2,1)S(1)}, u32[]{:S(2)}, u32[]{:S(2)}) %collective-permute-start.13) | collective-permute-done | bytes 368672 | tf_op jit(solution)/shard_map/ppermute | solution.py:34
  99.2 2.6 %collective-permute-start.14 = (bf16[384,640]{1,0:T(8,128)(2,1)S(1)}, bf16[384,640]{1,0:T(8,128)(2,1)S(1)}, u32[]{:S(2)}, u32[]{:S(2)}) collective-permute-start(bf16[384,640]{1,0:T(8,128)(2,1)S(1)} %shard_map.51), channel_id=1, source_target_pairs={{0,8},{1,9},{2,10},{3,11},{4,12},{5,13},{6,14},{7,15},{64,72},{65,... | collective-permute-start | bytes 1474568 | tf_op jit(solution)/shard_map/ppermute | solution.py:34
  101.9 0.0 collective-permute-done.19.refs_3_
  101.9 3.0 %collective-permute-start.17 = (bf16[384,640]{1,0:T(8,128)(2,1)S(1)}, bf16[384,640]{1,0:T(8,128)(2,1)S(1)}, u32[]{:S(2)}, u32[]{:S(2)}) collective-permute-start(bf16[384,640]{1,0:T(8,128)(2,1)S(1)} %shard_map.54.refs_7_), channel_id=1, source_target_pairs={{0,6},{1,7},{2,4},{3,5},{4,2},{5,3},{6,0},{7,1},{64,70},{65,71},{6... | collective-permute-start | bytes 1474568 | tf_op jit(solution)/shard_map/ppermute | solution.py:34
  104.9 0.0 collective-permute-done.16.refs_8_
  104.9 0.1 collective-permute-start.18
  105.0 4.6 %shard_map.49 = (bf16[768,640]{1,0:T(8,128)(2,1)S(1)}, bf16[384,640]{1,0:T(8,128)(2,1)S(1)}, bf16[288,640]{1,0:T(8,128)(2,1)S(1)}) custom-call(s32[36]{0:T(128)S(1)} %scalars.1.refs_0_.meta, bf16[768,2560]{1,0:T(8,128)(2,1)S(1)} %stage.1.refs_1_, bf16[2560,1920]{1,0:T(8,128)(2,1)} %refs_2_.7, bf16[640,640]{1,0:T(8,128)(2,1)S(1)} %collective-permute-done.1.refs_3_, ...), custom_call_target="tpu_custom_call" | custom-call | flops 2516582400 | bytes 9175040 | tf_op jit(solution)/shard_map/pallas_call | solution.py:255
  109.6 4.8 %shard_map.55 = (f32[5,768,128]{2,1,0:T(8,128)S(1)}, f32[5,768,128]{2,1,0:T(8,128)S(1)}, f32[5,768,128]{2,1,0:T(8,128)S(1)}) custom-call(s32[36]{0:T(128)S(1)} %scalars.1.refs_0_.meta, bf16[768,640]{1,0:T(8,128)(2,1)S(1)} %get-tuple-element.30.refs_1_, bf16[768,640]{1,0:T(8,128)(2,1)S(1)} %get-tuple-element.31.refs_2_, ...), custom_call_target="tpu_custom_call" | custom-call | flops 1509949440 | bytes 2949120 | tf_op jit(solution)/shard_map/pallas_call | solution.py:346
  114.4 0.0 collective-permute-done.20.refs_5_
  114.4 3.4 %shard_map.56 = (f32[5,768,128]{2,1,0:T(8,128)S(1)}, f32[5,768,128]{2,1,0:T(8,128)S(1)}, f32[5,768,128]{2,1,0:T(8,128)S(1)}) custom-call(s32[36]{0:T(128)S(1)} %scalars.1.refs_0_.meta, bf16[384,640]{1,0:T(8,128)(2,1)S(1)} %get-tuple-element.27.refs_1_, ...), custom_call_target="tpu_custom_call", output_to_operand_aliasing={{0}: (6, {}), {1}: (7, {}), {2}: (8, {})} | custom-call | flops 754974720 | bytes 2457600 | tf_op jit(solution)/shard_map/pallas_call | solution.py:346
  117.8 0.0 collective-permute-done.14.refs_6_
  117.8 0.0 collective-permute-done.17.refs_9_
  117.8 8.5 %collective-permute-done.18.refs_10_ = bf16[384,640]{1,0:T(8,128)(2,1)S(1)} collective-permute-done((bf16[384,640]{1,0:T(8,128)(2,1)S(1)}, bf16[384,640]{1,0:T(8,128)(2,1)S(1)}, u32[]{:S(2)}, u32[]{:S(2)}) %collective-permute-start.18) | collective-permute-done | bytes 491552 | tf_op jit(solution)/shard_map/ppermute | solution.py:34
  126.3 4.8 %shard_map.57 = (bf16[384,640]{1,0:T(8,128)(2,1)S(1)}, bf16[384,640]{1,0:T(8,128)(2,1)S(1)}, f32[5,768,128]{2,1,0:T(8,128)S(1)}, f32[5,768,128]{2,1,0:T(8,128)S(1)}, f32[5,768,128]{2,1,0:T(8,128)S(1)}) custom-call(s32[36]{0:T(128)S(1)} %scalars.1.refs_0_.meta, ...), custom_call_target="tpu_custom_call", output_to_operand_aliasing={{2}: (11, {}), {3}: (12, {}), {4}: (13, {})} | custom-call | flops 566231040 | bytes 2334720 | tf_op jit(solution)/shard_map/pallas_call | solution.py:346
  131.1 1.6 %collective-permute-start.21 = (bf16[384,640]{1,0:T(8,128)(2,1)S(1)}, bf16[384,640]{1,0:T(8,128)(2,1)S(1)}, u32[]{:S(2)}, u32[]{:S(2)}) collective-permute-start(bf16[384,640]{1,0:T(8,128)(2,1)S(1)} %get-tuple-element.39), channel_id=1, source_target_pairs={{0,1},{1,0},{2,3},{3,2},{4,5},{5,4},{6,7},{7,6},{64,65},{65,64},{6... | collective-permute-start | bytes 1474568 | tf_op jit(solution)/shard_map/ppermute | solution.py:34
  132.7 2.4 %shard_map.59.part = f32[4,384,640]{2,1,0:T(8,128)S(1)} custom-call(s32[36]{0:T(128)S(1)} %scalars.1.refs_0_.meta, bf16[384,640]{1,0:T(8,128)(2,1)S(1)} %get-tuple-element.40.att, bf16[1280,1280]{1,0:T(8,128)(2,1)S(1)} %copy-done, bf16[640,1280]{1,0:T(8,128)(2,1)S(1)} %collective-permute-done.22.rem), custom_call_target="tpu_custom_call" | custom-call | flops 1258291200 | bytes 5242880 | tf_op jit(solution)/shard_map/pallas_call | solution.py:385
  135.2 0.0 collective-permute-done.21.att
  135.2 3.3 %shard_map.60 = bf16[384,2560]{1,0:T(8,128)(2,1)} custom-call(s32[36]{0:T(128)S(1)} %scalars.1.refs_0_.meta, bf16[384,640]{1,0:T(8,128)(2,1)S(1)} %collective-permute-done.21.att, bf16[1280,1280]{1,0:T(8,128)(2,1)S(1)} %copy-done, bf16[640,1280]{1,0:T(8,128)(2,1)S(1)} %collective-permute-done.23.rem, f32[4,384,640]{2,1,0:T(8,128)S(1)} %shard_map.59.part), custom_call_target="tpu_custom_call" | custom-call | flops 1258291200 | bytes 5242880 | tf_op jit(solution)/shard_map/pallas_call | solution.py:385
  (9 shorter events, 0.1 us)
Async XLA Ops:
  1.4 40.3 %collective-permute-start.9 = (bf16[1280,640]{1,0:T(8,128)(2,1)S(1)}, bf16[1280,640]{1,0:T(8,128)(2,1)S(1)}, u32[]{:S(2)}, u32[]{:S(2)}) collective-permute-start(bf16[1280,640]{1,0:T(8,128)(2,1)S(1)} %shard_map.48), channel_id=1, source_target_pairs={{0,72},{1,65},{2,74},{3,67},{4,76},{5,69},{6,78},{7,71},{64,0},{65... | collective-permute-start | bytes 4915208 | tf_op jit(solution)/shard_map/ppermute | solution.py:34
  4.0 2.5 %copy-start.2 = (bf16[1,384,2560]{2,1,0:T(8,128)(2,1)S(1)}, bf16[1,384,2560]{2,1,0:T(8,128)(2,1)}, u32[]{:S(2)}) copy-start(bf16[1,384,2560]{2,1,0:T(8,128)(2,1)} %param.4) | copy-start | bytes 5898244
  4.0 26.6 %collective-permute-start.1 = (bf16[640,640]{1,0:T(8,128)(2,1)S(1)}, bf16[640,640]{1,0:T(8,128)(2,1)S(1)}, u32[]{:S(2)}, u32[]{:S(2)}) collective-permute-start(bf16[640,640]{1,0:T(8,128)(2,1)S(1)} %shard_map.46), channel_id=1, source_target_pairs={{0,72},{1,65},{2,74},{3,67},{4,76},{5,69},{6,78},{7,71},{64,0},{65... | collective-permute-start | bytes 2457608 | tf_op jit(solution)/shard_map/ppermute | solution.py:34
  6.2 33.1 %collective-permute-start.2 = (bf16[640,640]{1,0:T(8,128)(2,1)S(1)}, bf16[640,640]{1,0:T(8,128)(2,1)S(1)}, u32[]{:S(2)}, u32[]{:S(2)}) collective-permute-start(bf16[640,640]{1,0:T(8,128)(2,1)S(1)} %shard_map.47), channel_id=1, source_target_pairs={{0,72},{1,65},{2,74},{3,67},{4,76},{5,69},{6,78},{7,71},{64,0},{65... | collective-permute-start | bytes 2457608 | tf_op jit(solution)/shard_map/ppermute | solution.py:34
  6.4 48.5 %copy-start.1 = (s32[4,10]{1,0:T(4,128)S(1)}, s32[4,10]{1,0:T(4,128)}, u32[]{:S(2)}) copy-start(s32[4,10]{1,0:T(4,128)} %offsets.1) | copy-start | bytes 484
  6.4 48.0 %collective-permute-start = (bf16[384,2560]{1,0:T(8,128)(2,1)S(1)}, bf16[384,2560]{1,0:T(8,128)(2,1)S(1)}, u32[]{:S(2)}, u32[]{:S(2)}) collective-permute-start(bf16[384,2560]{1,0:T(8,128)(2,1)S(1)} %bitcast.3), channel_id=1, source_target_pairs={{0,1},{1,0},{2,3},{3,2},{4,5},{5,4},{6,7},{7,6},{64,65},{65,64},{6... | collective-permute-start | bytes 5898248 | tf_op jit(solution)/shard_map/ppermute | solution.py:34
  30.6 12.6 %collective-permute-start.5 = (bf16[640,640]{1,0:T(8,128)(2,1)S(1)}, bf16[640,640]{1,0:T(8,128)(2,1)S(1)}, u32[]{:S(2)}, u32[]{:S(2)}) collective-permute-start(bf16[640,640]{1,0:T(8,128)(2,1)S(1)} %collective-permute-done.1.refs_3_), channel_id=1, source_target_pairs={{0,48},{1,17},{2,50},{3,19},{4,52},{5,21},{6,54},{7,23},{64,112},{... | collective-permute-start | bytes 2457608 | tf_op jit(solution)/shard_map/ppermute | solution.py:34
  39.3 11.5 %collective-permute-start.6 = (bf16[640,640]{1,0:T(8,128)(2,1)S(1)}, bf16[640,640]{1,0:T(8,128)(2,1)S(1)}, u32[]{:S(2)}, u32[]{:S(2)}) collective-permute-start(bf16[640,640]{1,0:T(8,128)(2,1)S(1)} %collective-permute-done.2.refs_4_), channel_id=1, source_target_pairs={{0,48},{1,17},{2,50},{3,19},{4,52},{5,21},{6,54},{7,23},{64,112},{... | collective-permute-start | bytes 2457608 | tf_op jit(solution)/shard_map/ppermute | solution.py:34
  39.5 14.9 %collective-permute-start.3 = (bf16[640,640]{1,0:T(8,128)(2,1)S(1)}, bf16[640,640]{1,0:T(8,128)(2,1)S(1)}, u32[]{:S(2)}, u32[]{:S(2)}) collective-permute-start(bf16[640,640]{1,0:T(8,128)(2,1)S(1)} %collective-permute-done.1.refs_3_), channel_id=1, source_target_pairs={{0,1},{1,0},{2,3},{3,2},{4,5},{5,4},{6,7},{7,6},{64,65},{65,64},{6... | collective-permute-start | bytes 2457608 | tf_op jit(solution)/shard_map/ppermute | solution.py:34
  41.7 27.6 %collective-permute-start.10 = (bf16[1280,640]{1,0:T(8,128)(2,1)S(1)}, bf16[1280,640]{1,0:T(8,128)(2,1)S(1)}, u32[]{:S(2)}, u32[]{:S(2)}) collective-permute-start(bf16[1280,640]{1,0:T(8,128)(2,1)S(1)} %collective-permute-done.9.refs_11_.refs_7_), channel_id=1, source_target_pairs={{0,1},{1,0},{2,3},{3,2},{4,5},{5,4},{6,7},{7,6},{64,65},{65,64},{6... | collective-permute-start | bytes 4915208 | tf_op jit(solution)/shard_map/ppermute | solution.py:34
  43.2 33.4 %collective-permute-start.22 = (bf16[640,1280]{1,0:T(8,128)(2,1)S(1)}, bf16[640,1280]{1,0:T(8,128)(2,1)S(1)}, u32[]{:S(2)}, u32[]{:S(2)}) collective-permute-start(bf16[640,1280]{1,0:T(8,128)(2,1)S(1)} %shard_map.58), channel_id=1, source_target_pairs={{0,72},{1,65},{2,74},{3,67},{4,76},{5,69},{6,78},{7,71},{64,0},{65... | collective-permute-start | bytes 4915208 | tf_op jit(solution)/shard_map/ppermute | solution.py:34
  50.8 7.5 %collective-permute-start.4 = (bf16[640,640]{1,0:T(8,128)(2,1)S(1)}, bf16[640,640]{1,0:T(8,128)(2,1)S(1)}, u32[]{:S(2)}, u32[]{:S(2)}) collective-permute-start(bf16[640,640]{1,0:T(8,128)(2,1)S(1)} %collective-permute-done.2.refs_4_), channel_id=1, source_target_pairs={{0,1},{1,0},{2,3},{3,2},{4,5},{5,4},{6,7},{7,6},{64,65},{65,64},{6... | collective-permute-start | bytes 2457608 | tf_op jit(solution)/shard_map/ppermute | solution.py:34
  54.4 14.8 %collective-permute-start.7 = (bf16[640,640]{1,0:T(8,128)(2,1)S(1)}, bf16[640,640]{1,0:T(8,128)(2,1)S(1)}, u32[]{:S(2)}, u32[]{:S(2)}) collective-permute-start(bf16[640,640]{1,0:T(8,128)(2,1)S(1)} %collective-permute-done.5.refs_7_.refs_5_), channel_id=1, source_target_pairs={{0,1},{1,0},{2,3},{3,2},{4,5},{5,4},{6,7},{7,6},{64,65},{65,64},{6... | collective-permute-start | bytes 2457608 | tf_op jit(solution)/shard_map/ppermute | solution.py:34
  54.4 1.7 %copy-start.3 = (bf16[384,2560]{1,0:T(8,128)(2,1)}, bf16[384,2560]{1,0:T(8,128)(2,1)S(1)}, u32[]{:S(2)}) copy-start(bf16[384,2560]{1,0:T(8,128)(2,1)S(1)} %collective-permute-done.x_oth) | copy-start | bytes 5898244
  54.4 14.8 %collective-permute-start.8 = (bf16[640,640]{1,0:T(8,128)(2,1)S(1)}, bf16[640,640]{1,0:T(8,128)(2,1)S(1)}, u32[]{:S(2)}, u32[]{:S(2)}) collective-permute-start(bf16[640,640]{1,0:T(8,128)(2,1)S(1)} %collective-permute-done.6.refs_8_.refs_6_), channel_id=1, source_target_pairs={{0,1},{1,0},{2,3},{3,2},{4,5},{5,4},{6,7},{7,6},{64,65},{65,64},{6... | collective-permute-start | bytes 2457608 | tf_op jit(solution)/shard_map/ppermute | solution.py:34
  63.8 18.7 %collective-permute-start.11 = (bf16[288,640]{1,0:T(8,128)(2,1)S(1)}, bf16[288,640]{1,0:T(8,128)(2,1)S(1)}, u32[]{:S(2)}, u32[]{:S(2)}) collective-permute-start(bf16[288,640]{1,0:T(8,128)(2,1)S(1)} %get-tuple-element.24.refs_0_.refs_2_), channel_id=1, source_target_pairs={{0,2},{1,3},{2,0},{3,1},{4,6},{5,7},{6,4},{7,5},{64,66},{65,67},{6... | collective-permute-start | bytes 1105928 | tf_op jit(solution)/shard_map/ppermute | solution.py:34
  73.2 5.6 %collective-permute-start.15 = (bf16[96,640]{1,0:T(8,128)(2,1)S(1)}, bf16[96,640]{1,0:T(8,128)(2,1)S(1)}, u32[]{:S(2)}, u32[]{:S(2)}) collective-permute-start(bf16[96,640]{1,0:T(8,128)(2,1)S(1)} %get-tuple-element.25), channel_id=1, source_target_pairs={{0,8},{1,9},{2,10},{3,11},{4,12},{5,13},{6,14},{7,15},{64,72},{65,... | collective-permute-start | bytes 368648 | tf_op jit(solution)/shard_map/ppermute | solution.py:34
  76.6 58.6 %collective-permute-start.23 = (bf16[640,1280]{1,0:T(8,128)(2,1)S(1)}, bf16[640,1280]{1,0:T(8,128)(2,1)S(1)}, u32[]{:S(2)}, u32[]{:S(2)}) collective-permute-start(bf16[640,1280]{1,0:T(8,128)(2,1)S(1)} %collective-permute-done.22.rem), channel_id=1, source_target_pairs={{0,1},{1,0},{2,3},{3,2},{4,5},{5,4},{6,7},{7,6},{64,65},{65,64},{6... | collective-permute-start | bytes 4915208 | tf_op jit(solution)/shard_map/ppermute | solution.py:34
  76.6 25.3 %collective-permute-start.19 = (bf16[384,640]{1,0:T(8,128)(2,1)S(1)}, bf16[384,640]{1,0:T(8,128)(2,1)S(1)}, u32[]{:S(2)}, u32[]{:S(2)}) collective-permute-start(bf16[384,640]{1,0:T(8,128)(2,1)S(1)} %get-tuple-element.28.refs_2_), channel_id=1, source_target_pairs={{0,2},{1,3},{2,0},{3,1},{4,6},{5,7},{6,4},{7,5},{64,66},{65,67},{6... | collective-permute-start | bytes 1474568 | tf_op jit(solution)/shard_map/ppermute | solution.py:34
  78.8 26.0 %collective-permute-start.16 = (bf16[384,640]{1,0:T(8,128)(2,1)S(1)}, bf16[384,640]{1,0:T(8,128)(2,1)S(1)}, u32[]{:S(2)}, u32[]{:S(2)}) collective-permute-start(bf16[384,640]{1,0:T(8,128)(2,1)S(1)} %shard_map.54.refs_7_), channel_id=1, source_target_pairs={{0,2},{1,3},{2,0},{3,1},{4,6},{5,7},{6,4},{7,5},{64,66},{65,67},{6... | collective-permute-start | bytes 1474568 | tf_op jit(solution)/shard_map/ppermute | solution.py:34
  78.9 12.7 %collective-permute-start.12 = (bf16[288,640]{1,0:T(8,128)(2,1)S(1)}, bf16[288,640]{1,0:T(8,128)(2,1)S(1)}, u32[]{:S(2)}, u32[]{:S(2)}) collective-permute-start(bf16[288,640]{1,0:T(8,128)(2,1)S(1)} %get-tuple-element.24.refs_0_.refs_2_), channel_id=1, source_target_pairs={{0,6},{1,7},{2,4},{3,5},{4,2},{5,3},{6,0},{7,1},{64,70},{65,71},{6... | collective-permute-start | bytes 1105928 | tf_op jit(solution)/shard_map/ppermute | solution.py:34
  82.5 16.7 %collective-permute-start.13 = (bf16[288,640]{1,0:T(8,128)(2,1)S(1)}, bf16[288,640]{1,0:T(8,128)(2,1)S(1)}, u32[]{:S(2)}, u32[]{:S(2)}) collective-permute-start(bf16[288,640]{1,0:T(8,128)(2,1)S(1)} %collective-permute-done.11.refs_1_.refs_3_), channel_id=1, source_target_pairs={{0,6},{1,7},{2,4},{3,5},{4,2},{5,3},{6,0},{7,1},{64,70},{65,71},{6... | collective-permute-start | bytes 1105928 | tf_op jit(solution)/shard_map/ppermute | solution.py:34
  91.7 22.8 %collective-permute-start.20 = (bf16[384,640]{1,0:T(8,128)(2,1)S(1)}, bf16[384,640]{1,0:T(8,128)(2,1)S(1)}, u32[]{:S(2)}, u32[]{:S(2)}) collective-permute-start(bf16[384,640]{1,0:T(8,128)(2,1)S(1)} %get-tuple-element.29.refs_4_), channel_id=1, source_target_pairs={{0,2},{1,3},{2,0},{3,1},{4,6},{5,7},{6,4},{7,5},{64,66},{65,67},{6... | collective-permute-start | bytes 1474568 | tf_op jit(solution)/shard_map/ppermute | solution.py:34
  99.2 18.6 %collective-permute-start.14 = (bf16[384,640]{1,0:T(8,128)(2,1)S(1)}, bf16[384,640]{1,0:T(8,128)(2,1)S(1)}, u32[]{:S(2)}, u32[]{:S(2)}) collective-permute-start(bf16[384,640]{1,0:T(8,128)(2,1)S(1)} %shard_map.51), channel_id=1, source_target_pairs={{0,8},{1,9},{2,10},{3,11},{4,12},{5,13},{6,14},{7,15},{64,72},{65,... | collective-permute-start | bytes 1474568 | tf_op jit(solution)/shard_map/ppermute | solution.py:34
  101.9 16.0 %collective-permute-start.17 = (bf16[384,640]{1,0:T(8,128)(2,1)S(1)}, bf16[384,640]{1,0:T(8,128)(2,1)S(1)}, u32[]{:S(2)}, u32[]{:S(2)}) collective-permute-start(bf16[384,640]{1,0:T(8,128)(2,1)S(1)} %shard_map.54.refs_7_), channel_id=1, source_target_pairs={{0,6},{1,7},{2,4},{3,5},{4,2},{5,3},{6,0},{7,1},{64,70},{65,71},{6... | collective-permute-start | bytes 1474568 | tf_op jit(solution)/shard_map/ppermute | solution.py:34
  104.9 21.5 %collective-permute-start.18 = (bf16[384,640]{1,0:T(8,128)(2,1)S(1)}, bf16[384,640]{1,0:T(8,128)(2,1)S(1)}, u32[]{:S(2)}, u32[]{:S(2)}) collective-permute-start(bf16[384,640]{1,0:T(8,128)(2,1)S(1)} %collective-permute-done.16.refs_8_), channel_id=1, source_target_pairs={{0,6},{1,7},{2,4},{3,5},{4,2},{5,3},{6,0},{7,1},{64,70},{65,71},{6... | collective-permute-start | bytes 1474568 | tf_op jit(solution)/shard_map/ppermute | solution.py:34
  126.3 6.3 %copy-start = (bf16[1280,1280]{1,0:T(8,128)(2,1)S(1)}, bf16[1280,1280]{1,0:T(8,128)(2,1)}, u32[]{:S(2)}) copy-start(bf16[1280,1280]{1,0:T(8,128)(2,1)} %w_loc.3) | copy-start | bytes 9830404
  131.1 4.0 %collective-permute-start.21 = (bf16[384,640]{1,0:T(8,128)(2,1)S(1)}, bf16[384,640]{1,0:T(8,128)(2,1)S(1)}, u32[]{:S(2)}, u32[]{:S(2)}) collective-permute-start(bf16[384,640]{1,0:T(8,128)(2,1)S(1)} %get-tuple-element.39), channel_id=1, source_target_pairs={{0,1},{1,0},{2,3},{3,2},{4,5},{5,4},{6,7},{7,6},{64,65},{65,64},{6... | collective-permute-start | bytes 1474568 | tf_op jit(solution)/shard_map/ppermute | solution.py:34

commit v3 on v2

--- a/solution.py
+++ b/solution.py
@@ -356,26 +356,32 @@
     )(meta, *held(*arrays))
 
 
-def tile_of(t, core_rows, w_loc, rem):
-    cols = pl.ds((t % 2) * WB, WB)
-    return w_loc[core_rows, cols] if t < 2 else rem[:, cols]
+TILES = tuple((side, low, wide) for side in range(2) for low, wide in ((0, 768), (768, 512)))
+
+
+def tile_of(tile, core_rows, w_loc, rem):
+    side, low, wide = tile
+    return w_loc[core_rows, pl.ds(low, wide)] if side == 0 else rem[:, pl.ds(low, wide)]
 
 
 def out_own_kernel(meta, att, w_loc, rem, part):
     rows = pl.ds(pl.multiple_of(meta[META_CORE] * WB, HD), WB)
-    for t in range(4):
-        part[t] = jnp.dot(att[...], tile_of(t, rows, w_loc, rem), preferred_element_type=jnp.float32)
+    for tile in TILES:
+        cols = pl.ds(tile[0] * 2 * WB + tile[1], tile[2])
+        part[:, cols] = jnp.dot(att[...], tile_of(tile, rows, w_loc, rem), preferred_element_type=jnp.float32)
 
 
 def out_oth_kernel(meta, att, w_loc, rem, part, out, buf, sem):
     rows = pl.ds(pl.multiple_of((1 - meta[META_CORE]) * WB, HD), WB)
     d = meta[META_DP]
     copies = []
-    for t in range(4):
-        got = part[t] + jnp.dot(att[...], tile_of(t, rows, w_loc, rem), preferred_element_type=jnp.float32)
-        buf[t] = got.astype(jnp.bfloat16)
-        col = (d if t < 2 else 1 - d) * (2 * WB) + (t % 2) * WB
-        copies.append(pltpu.make_async_copy(buf.at[t], out.at[:, pl.ds(pl.multiple_of(col, HD), WB)], sem.at[t]))
+    for n, tile in enumerate(TILES):
+        side, low, wide = tile
+        cols = pl.ds(side * 2 * WB + low, wide)
+        got = part[:, cols] + jnp.dot(att[...], tile_of(tile, rows, w_loc, rem), preferred_element_type=jnp.float32)
+        buf[:, cols] = got.astype(jnp.bfloat16)
+        to = (d if side == 0 else 1 - d) * (2 * WB) + low
+        copies.append(pltpu.make_async_copy(buf.at[:, cols], out.at[:, pl.ds(pl.multiple_of(to, HD), wide)], sem.at[n]))
         copies[-1].start()
     for copy in copies:
         copy.wait()
@@ -444,7 +450,7 @@
     att, att_send, *_ = attend(level23_kernel, meta, arrays, outs, CUT3, {11: 2, 12: 3, 13: 4})
     att_oth = send(att_send, to_core)
     part = out_project(
-        out_own_kernel, meta, [att, out_weight, rem_own], pltpu.VMEM((4, TOK, WB), jnp.float32), HELD, []
+        out_own_kernel, meta, [att, out_weight, rem_own], pltpu.VMEM((TOK, 4 * WB), jnp.float32), HELD, []
     )
     mixed = out_project(
         out_oth_kernel,
@@ -452,7 +458,7 @@
         [att_oth, out_weight, rem_oth, part],
         jax.ShapeDtypeStruct((TOK, 4 * WB), jnp.bfloat16),
         FAR,
-        [pltpu.VMEM((4, TOK, WB), jnp.bfloat16), pltpu.SemaphoreType.DMA((4,))],
+        [pltpu.VMEM((TOK, 4 * WB), jnp.bfloat16), pltpu.SemaphoreType.DMA((len(TILES),))],
     )
     return mixed.reshape(1, TOK, mixed.shape[1])
 

time: 139 us -> 139 us (level)
  no operation moved by 1% of the time
where the time goes in v3:
time: 139 us; the launch traced here: 138 us
  waiting for transfers between devices  64 us (46%)
  Pallas kernels  44.7 us (32%)
  starting transfers between devices  29.1 us (21%)
    ppermute x24, waiting for transfers between devices, send(): return lax.ppermute(block, ('dp', 'ctx'), route)  64 us
    ppermute x24, starting transfers between devices, send(): return lax.ppermute(block, ('dp', 'ctx'), route)  29.1 us
    pallas_call x4, Pallas kernels, project(): pl.pallas_call(lambda *refs: proj_kernel([len(g) for g in groups], slot,...  17.8 us
    pallas_call x3, Pallas kernels, attend(): pl.pallas_call(lambda *refs: kernel(factor, *refs), out_shape=[pltpu.VMEM...  13 us
    pallas_call x2, Pallas kernels, out_project(): pl.pallas_call(kernel, out_shape=out_shape, in_specs=[SCALARS] + [HELD] *...  5.38 us
    pallas_call x4, Pallas kernels, payload(): pl.pallas_call(lambda *refs: payload_kernel(block, part, parts, *refs), o...  5.18 us
  transfers between devices with their start and end apart: 24, of which 7 were waited for; matrix products, arithmetic and copies ran while one was open for 0% of the time, Pallas kernels for 29%

profile of v3, /device:TPU:15, one launch (start us, length us, event | category | flops | bytes accessed | tf_op | source)
XLA Modules:
  0.0 138.3 jit_solution(2679790003863163165)
XLA Ops:
  0.0 1.4 %shard_map.48 = bf16[1280,640]{1,0:T(8,128)(2,1)S(1)} custom-call(bf16[2560,1920]{1,0:T(8,128)(2,1)} %refs_2_.7), custom_call_target="tpu_custom_call" | custom-call | tf_op jit(solution)/shard_map/pallas_call | solution.py:165
  1.4 1.4 collective-permute-start.9
  2.8 1.2 shard_map.46
  4.0 0.0 copy-start.2
  4.0 1.1 collective-permute-start.1
  5.1 1.2 shard_map.47
  6.2 0.2 collective-permute-start.2
  6.4 2.4 %collective-permute-start = (bf16[384,2560]{1,0:T(8,128)(2,1)S(1)}, bf16[384,2560]{1,0:T(8,128)(2,1)S(1)}, u32[]{:S(2)}, u32[]{:S(2)}) collective-permute-start(bf16[384,2560]{1,0:T(8,128)(2,1)S(1)} %bitcast.3), channel_id=1, source_target_pairs={{0,1},{1,0},{2,3},{3,2},{4,5},{5,4},{6,7},{7,6},{64,65},{65,64},{6... | collective-permute-start | bytes 5898248 | tf_op jit(solution)/shard_map/ppermute | solution.py:34
  8.9 21.7 %collective-permute-done.1.refs_3_ = bf16[640,640]{1,0:T(8,128)(2,1)S(1)} collective-permute-done((bf16[640,640]{1,0:T(8,128)(2,1)S(1)}, bf16[640,640]{1,0:T(8,128)(2,1)S(1)}, u32[]{:S(2)}, u32[]{:S(2)}) %collective-permute-start.1) | collective-permute-done | bytes 819232 | tf_op jit(solution)/shard_map/ppermute | solution.py:34
  30.6 0.2 collective-permute-start.5
  30.8 8.6 %collective-permute-done.2.refs_4_ = bf16[640,640]{1,0:T(8,128)(2,1)S(1)} collective-permute-done((bf16[640,640]{1,0:T(8,128)(2,1)S(1)}, bf16[640,640]{1,0:T(8,128)(2,1)S(1)}, u32[]{:S(2)}, u32[]{:S(2)}) %collective-permute-start.2) | collective-permute-done | bytes 819232 | tf_op jit(solution)/shard_map/ppermute | solution.py:34
  39.3 0.2 collective-permute-start.6
  39.5 2.2 %collective-permute-start.3 = (bf16[640,640]{1,0:T(8,128)(2,1)S(1)}, bf16[640,640]{1,0:T(8,128)(2,1)S(1)}, u32[]{:S(2)}, u32[]{:S(2)}) collective-permute-start(bf16[640,640]{1,0:T(8,128)(2,1)S(1)} %collective-permute-done.1.refs_3_), channel_id=1, source_target_pairs={{0,1},{1,0},{2,3},{3,2},{4,5},{5,4},{6,7},{7,6},{64,65},{65,64},{6... | collective-permute-start | bytes 2457608 | tf_op jit(solution)/shard_map/ppermute | solution.py:34
  41.7 0.0 collective-permute-done.9.refs_11_.refs_7_
  41.7 0.0 collective-permute-start.10
  41.7 1.4 %shard_map.58 = bf16[640,1280]{1,0:T(8,128)(2,1)S(1)} custom-call(bf16[1280,1280]{1,0:T(8,128)(2,1)} %w_loc.3), custom_call_target="tpu_custom_call" | custom-call | tf_op jit(solution)/shard_map/pallas_call | solution.py:165
  43.1 0.0 collective-permute-done.5.refs_7_.refs_5_
  43.2 1.4 collective-permute-start.22
  44.5 6.3 %collective-permute-done.6.refs_8_.refs_6_ = bf16[640,640]{1,0:T(8,128)(2,1)S(1)} collective-permute-done((bf16[640,640]{1,0:T(8,128)(2,1)S(1)}, bf16[640,640]{1,0:T(8,128)(2,1)S(1)}, u32[]{:S(2)}, u32[]{:S(2)}) %collective-permute-start.6) | collective-permute-done | bytes 819232 | tf_op jit(solution)/shard_map/ppermute | solution.py:34
  50.8 3.6 %collective-permute-start.4 = (bf16[640,640]{1,0:T(8,128)(2,1)S(1)}, bf16[640,640]{1,0:T(8,128)(2,1)S(1)}, u32[]{:S(2)}, u32[]{:S(2)}) collective-permute-start(bf16[640,640]{1,0:T(8,128)(2,1)S(1)} %collective-permute-done.2.refs_4_), channel_id=1, source_target_pairs={{0,1},{1,0},{2,3},{3,2},{4,5},{5,4},{6,7},{7,6},{64,65},{65,64},{6... | collective-permute-start | bytes 2457608 | tf_op jit(solution)/shard_map/ppermute | solution.py:34
  54.4 0.0 collective-permute-done.3.refs_5_.refs_3_
  54.4 0.0 collective-permute-start.7
  54.4 0.0 collective-permute-done.x_oth
  54.4 0.0 copy-start.3
  54.4 0.5 collective-permute-start.8
  54.9 1.2 scalars.1.refs_0_.meta
  56.2 2.2 %stage.1.refs_1_ = bf16[768,2560]{1,0:T(8,128)(2,1)S(1)} custom-call(bf16[384,2560]{1,0:T(8,128)(2,1)} %bitcast.2, bf16[384,2560]{1,0:T(8,128)(2,1)} %copy-done.3), custom_call_target="tpu_custom_call" | custom-call | tf_op jit(solution)/shard_map/stage/pallas_call | solution.py:113
  58.3 0.0 collective-permute-done.4.refs_6_.refs_4_
  58.3 5.5 %shard_map.50 = (bf16[768,640]{1,0:T(8,128)(2,1)S(1)}, bf16[384,640]{1,0:T(8,128)(2,1)S(1)}, bf16[288,640]{1,0:T(8,128)(2,1)S(1)}) custom-call(s32[36]{0:T(128)S(1)} %scalars.1.refs_0_.meta, bf16[768,2560]{1,0:T(8,128)(2,1)S(1)} %stage.1.refs_1_, bf16[2560,1920]{1,0:T(8,128)(2,1)} %refs_2_.7, bf16[640,640]{1,0:T(8,128)(2,1)S(1)} %collective-permute-done.1.refs_3_, ...), custom_call_target="tpu_custom_call" | custom-call | flops 2516582400 | bytes 9175040 | tf_op jit(solution)/shard_map/pallas_call | solution.py:255
  63.8 1.7 %collective-permute-start.11 = (bf16[288,640]{1,0:T(8,128)(2,1)S(1)}, bf16[288,640]{1,0:T(8,128)(2,1)S(1)}, u32[]{:S(2)}, u32[]{:S(2)}) collective-permute-start(bf16[288,640]{1,0:T(8,128)(2,1)S(1)} %get-tuple-element.24.refs_0_.refs_2_), channel_id=1, source_target_pairs={{0,2},{1,3},{2,0},{3,1},{4,6},{5,7},{6,4},{7,5},{64,66},{65,67},{6... | collective-permute-start | bytes 1105928 | tf_op jit(solution)/shard_map/ppermute | solution.py:34
  65.6 3.7 %shard_map.52.refs_8_ = f32[5,768,128]{2,1,0:T(8,128)S(1)} custom-call(s32[36]{0:T(128)S(1)} %scalars.1.refs_0_.meta, bf16[768,2560]{1,0:T(8,128)(2,1)S(1)} %stage.1.refs_1_, bf16[2560,1920]{1,0:T(8,128)(2,1)} %refs_2_.7, bf16[640,640]{1,0:T(8,128)(2,1)S(1)} %collective-permute-done.1.refs_3_, bf16[640,640]{1,0:T(8,128)(2,1)S(1)} %collective-permute-done.2.refs_4_, ...), custom_call_target="tpu_custom_call" | custom-call | flops 1258291200 | bytes 9175040 | tf_op jit(solution)/shard_map/pallas_call | solution.py:255
  69.2 0.0 collective-permute-done.7.refs_9_.refs_5_
  69.2 0.0 collective-permute-done.8.refs_10_.refs_6_
  69.3 0.0 collective-permute-done.10.refs_12_.refs_7_
  69.3 4.0 %shard_map.53 = (bf16[768,640]{1,0:T(8,128)(2,1)S(1)}, bf16[384,640]{1,0:T(8,128)(2,1)S(1)}, bf16[384,640]{1,0:T(8,128)(2,1)S(1)}, bf16[96,640]{1,0:T(8,128)(2,1)S(1)}) custom-call(s32[36]{0:T(128)S(1)} %scalars.1.refs_0_.meta, bf16[768,2560]{1,0:T(8,128)(2,1)S(1)} %stage.1.refs_1_, bf16[2560,1920]{1,0:T(8,128)(2,1)} %refs_2_.7, ...), custom_call_target="tpu_custom_call" | custom-call | flops 1258291200 | bytes 9175040 | tf_op jit(solution)/shard_map/pallas_call | solution.py:255
  73.2 3.3 %collective-permute-start.15 = (bf16[96,640]{1,0:T(8,128)(2,1)S(1)}, bf16[96,640]{1,0:T(8,128)(2,1)S(1)}, u32[]{:S(2)}, u32[]{:S(2)}) collective-permute-start(bf16[96,640]{1,0:T(8,128)(2,1)S(1)} %get-tuple-element.25), channel_id=1, source_target_pairs={{0,8},{1,9},{2,10},{3,11},{4,12},{5,13},{6,14},{7,15},{64,72},{65,... | collective-permute-start | bytes 368648 | tf_op jit(solution)/shard_map/ppermute | solution.py:34
  76.6 0.0 collective-permute-done.22.rem
  76.6 0.0 collective-permute-start.23
  76.6 0.0 collective-permute-start.19
  76.6 2.2 %collective-permute-done.15.far_rows = bf16[96,640]{1,0:T(8,128)(2,1)S(1)} collective-permute-done((bf16[96,640]{1,0:T(8,128)(2,1)S(1)}, bf16[96,640]{1,0:T(8,128)(2,1)S(1)}, u32[]{:S(2)}, u32[]{:S(2)}) %collective-permute-start.15) | collective-permute-done | bytes 122912 | tf_op jit(solution)/shard_map/ppermute | solution.py:34
  78.8 0.1 collective-permute-start.16
  78.9 3.6 %collective-permute-start.12 = (bf16[288,640]{1,0:T(8,128)(2,1)S(1)}, bf16[288,640]{1,0:T(8,128)(2,1)S(1)}, u32[]{:S(2)}, u32[]{:S(2)}) collective-permute-start(bf16[288,640]{1,0:T(8,128)(2,1)S(1)} %get-tuple-element.24.refs_0_.refs_2_), channel_id=1, source_target_pairs={{0,6},{1,7},{2,4},{3,5},{4,2},{5,3},{6,0},{7,1},{64,70},{65,71},{6... | collective-permute-start | bytes 1105928 | tf_op jit(solution)/shard_map/ppermute | solution.py:34
  82.5 0.0 collective-permute-done.11.refs_1_.refs_3_
  82.5 0.0 collective-permute-start.13
  82.5 9.1 %collective-permute-done.12.refs_2_.refs_4_ = bf16[288,640]{1,0:T(8,128)(2,1)S(1)} collective-permute-done((bf16[288,640]{1,0:T(8,128)(2,1)S(1)}, bf16[288,640]{1,0:T(8,128)(2,1)S(1)}, u32[]{:S(2)}, u32[]{:S(2)}) %collective-permute-start.12) | collective-permute-done | bytes 368672 | tf_op jit(solution)/shard_map/ppermute | solution.py:34
  91.7 0.0 collective-permute-start.20
  91.7 7.5 %collective-permute-done.13.refs_3_.refs_5_ = bf16[288,640]{1,0:T(8,128)(2,1)S(1)} collective-permute-done((bf16[288,640]{1,0:T(8,128)(2,1)S(1)}, bf16[288,640]{1,0:T(8,128)(2,1)S(1)}, u32[]{:S(2)}, u32[]{:S(2)}) %collective-permute-start.13) | collective-permute-done | bytes 368672 | tf_op jit(solution)/shard_map/ppermute | solution.py:34
  99.2 2.6 %collective-permute-start.14 = (bf16[384,640]{1,0:T(8,128)(2,1)S(1)}, bf16[384,640]{1,0:T(8,128)(2,1)S(1)}, u32[]{:S(2)}, u32[]{:S(2)}) collective-permute-start(bf16[384,640]{1,0:T(8,128)(2,1)S(1)} %shard_map.51), channel_id=1, source_target_pairs={{0,8},{1,9},{2,10},{3,11},{4,12},{5,13},{6,14},{7,15},{64,72},{65,... | collective-permute-start | bytes 1474568 | tf_op jit(solution)/shard_map/ppermute | solution.py:34
  101.9 0.0 collective-permute-done.19.refs_3_
  101.9 3.0 %collective-permute-start.17 = (bf16[384,640]{1,0:T(8,128)(2,1)S(1)}, bf16[384,640]{1,0:T(8,128)(2,1)S(1)}, u32[]{:S(2)}, u32[]{:S(2)}) collective-permute-start(bf16[384,640]{1,0:T(8,128)(2,1)S(1)} %shard_map.54.refs_7_), channel_id=1, source_target_pairs={{0,6},{1,7},{2,4},{3,5},{4,2},{5,3},{6,0},{7,1},{64,70},{65,71},{6... | collective-permute-start | bytes 1474568 | tf_op jit(solution)/shard_map/ppermute | solution.py:34
  104.9 0.0 collective-permute-done.16.refs_8_
  104.9 0.1 collective-permute-start.18
  105.0 4.6 %shard_map.49 = (bf16[768,640]{1,0:T(8,128)(2,1)S(1)}, bf16[384,640]{1,0:T(8,128)(2,1)S(1)}, bf16[288,640]{1,0:T(8,128)(2,1)S(1)}) custom-call(s32[36]{0:T(128)S(1)} %scalars.1.refs_0_.meta, bf16[768,2560]{1,0:T(8,128)(2,1)S(1)} %stage.1.refs_1_, bf16[2560,1920]{1,0:T(8,128)(2,1)} %refs_2_.7, bf16[640,640]{1,0:T(8,128)(2,1)S(1)} %collective-permute-done.1.refs_3_, ...), custom_call_target="tpu_custom_call" | custom-call | flops 2516582400 | bytes 9175040 | tf_op jit(solution)/shard_map/pallas_call | solution.py:255
  109.6 4.8 %shard_map.55 = (f32[5,768,128]{2,1,0:T(8,128)S(1)}, f32[5,768,128]{2,1,0:T(8,128)S(1)}, f32[5,768,128]{2,1,0:T(8,128)S(1)}) custom-call(s32[36]{0:T(128)S(1)} %scalars.1.refs_0_.meta, bf16[768,640]{1,0:T(8,128)(2,1)S(1)} %get-tuple-element.30.refs_1_, bf16[768,640]{1,0:T(8,128)(2,1)S(1)} %get-tuple-element.31.refs_2_, ...), custom_call_target="tpu_custom_call" | custom-call | flops 1509949440 | bytes 2949120 | tf_op jit(solution)/shard_map/pallas_call | solution.py:346
  114.4 0.0 collective-permute-done.20.refs_5_
  114.4 3.4 %shard_map.56 = (f32[5,768,128]{2,1,0:T(8,128)S(1)}, f32[5,768,128]{2,1,0:T(8,128)S(1)}, f32[5,768,128]{2,1,0:T(8,128)S(1)}) custom-call(s32[36]{0:T(128)S(1)} %scalars.1.refs_0_.meta, bf16[384,640]{1,0:T(8,128)(2,1)S(1)} %get-tuple-element.27.refs_1_, ...), custom_call_target="tpu_custom_call", output_to_operand_aliasing={{0}: (6, {}), {1}: (7, {}), {2}: (8, {})} | custom-call | flops 754974720 | bytes 2457600 | tf_op jit(solution)/shard_map/pallas_call | solution.py:346
  117.8 0.0 collective-permute-done.17.refs_9_
  117.8 8.5 %collective-permute-done.18.refs_10_ = bf16[384,640]{1,0:T(8,128)(2,1)S(1)} collective-permute-done((bf16[384,640]{1,0:T(8,128)(2,1)S(1)}, bf16[384,640]{1,0:T(8,128)(2,1)S(1)}, u32[]{:S(2)}, u32[]{:S(2)}) %collective-permute-start.18) | collective-permute-done | bytes 491552 | tf_op jit(solution)/shard_map/ppermute | solution.py:34
  126.3 4.8 %shard_map.57 = (bf16[384,640]{1,0:T(8,128)(2,1)S(1)}, bf16[384,640]{1,0:T(8,128)(2,1)S(1)}, f32[5,768,128]{2,1,0:T(8,128)S(1)}, f32[5,768,128]{2,1,0:T(8,128)S(1)}, f32[5,768,128]{2,1,0:T(8,128)S(1)}) custom-call(s32[36]{0:T(128)S(1)} %scalars.1.refs_0_.meta, ...), custom_call_target="tpu_custom_call", output_to_operand_aliasing={{2}: (11, {}), {3}: (12, {}), {4}: (13, {})} | custom-call | flops 566231040 | bytes 2334720 | tf_op jit(solution)/shard_map/pallas_call | solution.py:346
  131.1 1.6 %collective-permute-start.21 = (bf16[384,640]{1,0:T(8,128)(2,1)S(1)}, bf16[384,640]{1,0:T(8,128)(2,1)S(1)}, u32[]{:S(2)}, u32[]{:S(2)}) collective-permute-start(bf16[384,640]{1,0:T(8,128)(2,1)S(1)} %get-tuple-element.39), channel_id=1, source_target_pairs={{0,1},{1,0},{2,3},{3,2},{4,5},{5,4},{6,7},{7,6},{64,65},{65,64},{6... | collective-permute-start | bytes 1474568 | tf_op jit(solution)/shard_map/ppermute | solution.py:34
  132.7 2.2 %shard_map.59.part = f32[384,2560]{1,0:T(8,128)S(1)} custom-call(s32[36]{0:T(128)S(1)} %scalars.1.refs_0_.meta, bf16[384,640]{1,0:T(8,128)(2,1)S(1)} %get-tuple-element.40.att, bf16[1280,1280]{1,0:T(8,128)(2,1)S(1)} %copy-done, bf16[640,1280]{1,0:T(8,128)(2,1)S(1)} %collective-permute-done.22.rem), custom_call_target="tpu_custom_call" | custom-call | flops 1258291200 | bytes 5242880 | tf_op jit(solution)/shard_map/pallas_call | solution.py:391
  134.9 0.0 collective-permute-done.23.rem
  134.9 0.0 collective-permute-done.21.att
  134.9 3.1 %shard_map.60 = bf16[384,2560]{1,0:T(8,128)(2,1)} custom-call(s32[36]{0:T(128)S(1)} %scalars.1.refs_0_.meta, bf16[384,640]{1,0:T(8,128)(2,1)S(1)} %collective-permute-done.21.att, bf16[1280,1280]{1,0:T(8,128)(2,1)S(1)} %copy-done, bf16[640,1280]{1,0:T(8,128)(2,1)S(1)} %collective-permute-done.23.rem, f32[384,2560]{1,0:T(8,128)S(1)} %shard_map.59.part), custom_call_target="tpu_custom_call" | custom-call | flops 1258291200 | bytes 5242880 | tf_op jit(solution)/shard_map/pallas_call | solution.py:391
  (9 shorter events, 0.1 us)
Async XLA Ops:
  1.4 40.3 %collective-permute-start.9 = (bf16[1280,640]{1,0:T(8,128)(2,1)S(1)}, bf16[1280,640]{1,0:T(8,128)(2,1)S(1)}, u32[]{:S(2)}, u32[]{:S(2)}) collective-permute-start(bf16[1280,640]{1,0:T(8,128)(2,1)S(1)} %shard_map.48), channel_id=1, source_target_pairs={{0,72},{1,65},{2,74},{3,67},{4,76},{5,69},{6,78},{7,71},{64,0},{65... | collective-permute-start | bytes 4915208 | tf_op jit(solution)/shard_map/ppermute | solution.py:34
  4.0 2.5 %copy-start.2 = (bf16[1,384,2560]{2,1,0:T(8,128)(2,1)S(1)}, bf16[1,384,2560]{2,1,0:T(8,128)(2,1)}, u32[]{:S(2)}) copy-start(bf16[1,384,2560]{2,1,0:T(8,128)(2,1)} %param.4) | copy-start | bytes 5898244
  4.0 26.6 %collective-permute-start.1 = (bf16[640,640]{1,0:T(8,128)(2,1)S(1)}, bf16[640,640]{1,0:T(8,128)(2,1)S(1)}, u32[]{:S(2)}, u32[]{:S(2)}) collective-permute-start(bf16[640,640]{1,0:T(8,128)(2,1)S(1)} %shard_map.46), channel_id=1, source_target_pairs={{0,72},{1,65},{2,74},{3,67},{4,76},{5,69},{6,78},{7,71},{64,0},{65... | collective-permute-start | bytes 2457608 | tf_op jit(solution)/shard_map/ppermute | solution.py:34
  6.2 33.1 %collective-permute-start.2 = (bf16[640,640]{1,0:T(8,128)(2,1)S(1)}, bf16[640,640]{1,0:T(8,128)(2,1)S(1)}, u32[]{:S(2)}, u32[]{:S(2)}) collective-permute-start(bf16[640,640]{1,0:T(8,128)(2,1)S(1)} %shard_map.47), channel_id=1, source_target_pairs={{0,72},{1,65},{2,74},{3,67},{4,76},{5,69},{6,78},{7,71},{64,0},{65... | collective-permute-start | bytes 2457608 | tf_op jit(solution)/shard_map/ppermute | solution.py:34
  6.4 48.5 %copy-start.1 = (s32[4,10]{1,0:T(4,128)S(1)}, s32[4,10]{1,0:T(4,128)}, u32[]{:S(2)}) copy-start(s32[4,10]{1,0:T(4,128)} %offsets.1) | copy-start | bytes 484
  6.4 48.0 %collective-permute-start = (bf16[384,2560]{1,0:T(8,128)(2,1)S(1)}, bf16[384,2560]{1,0:T(8,128)(2,1)S(1)}, u32[]{:S(2)}, u32[]{:S(2)}) collective-permute-start(bf16[384,2560]{1,0:T(8,128)(2,1)S(1)} %bitcast.3), channel_id=1, source_target_pairs={{0,1},{1,0},{2,3},{3,2},{4,5},{5,4},{6,7},{7,6},{64,65},{65,64},{6... | collective-permute-start | bytes 5898248 | tf_op jit(solution)/shard_map/ppermute | solution.py:34
  30.6 12.6 %collective-permute-start.5 = (bf16[640,640]{1,0:T(8,128)(2,1)S(1)}, bf16[640,640]{1,0:T(8,128)(2,1)S(1)}, u32[]{:S(2)}, u32[]{:S(2)}) collective-permute-start(bf16[640,640]{1,0:T(8,128)(2,1)S(1)} %collective-permute-done.1.refs_3_), channel_id=1, source_target_pairs={{0,48},{1,17},{2,50},{3,19},{4,52},{5,21},{6,54},{7,23},{64,112},{... | collective-permute-start | bytes 2457608 | tf_op jit(solution)/shard_map/ppermute | solution.py:34
  39.3 11.5 %collective-permute-start.6 = (bf16[640,640]{1,0:T(8,128)(2,1)S(1)}, bf16[640,640]{1,0:T(8,128)(2,1)S(1)}, u32[]{:S(2)}, u32[]{:S(2)}) collective-permute-start(bf16[640,640]{1,0:T(8,128)(2,1)S(1)} %collective-permute-done.2.refs_4_), channel_id=1, source_target_pairs={{0,48},{1,17},{2,50},{3,19},{4,52},{5,21},{6,54},{7,23},{64,112},{... | collective-permute-start | bytes 2457608 | tf_op jit(solution)/shard_map/ppermute | solution.py:34
  39.5 14.9 %collective-permute-start.3 = (bf16[640,640]{1,0:T(8,128)(2,1)S(1)}, bf16[640,640]{1,0:T(8,128)(2,1)S(1)}, u32[]{:S(2)}, u32[]{:S(2)}) collective-permute-start(bf16[640,640]{1,0:T(8,128)(2,1)S(1)} %collective-permute-done.1.refs_3_), channel_id=1, source_target_pairs={{0,1},{1,0},{2,3},{3,2},{4,5},{5,4},{6,7},{7,6},{64,65},{65,64},{6... | collective-permute-start | bytes 2457608 | tf_op jit(solution)/shard_map/ppermute | solution.py:34
  41.7 27.6 %collective-permute-start.10 = (bf16[1280,640]{1,0:T(8,128)(2,1)S(1)}, bf16[1280,640]{1,0:T(8,128)(2,1)S(1)}, u32[]{:S(2)}, u32[]{:S(2)}) collective-permute-start(bf16[1280,640]{1,0:T(8,128)(2,1)S(1)} %collective-permute-done.9.refs_11_.refs_7_), channel_id=1, source_target_pairs={{0,1},{1,0},{2,3},{3,2},{4,5},{5,4},{6,7},{7,6},{64,65},{65,64},{6... | collective-permute-start | bytes 4915208 | tf_op jit(solution)/shard_map/ppermute | solution.py:34
  43.2 33.4 %collective-permute-start.22 = (bf16[640,1280]{1,0:T(8,128)(2,1)S(1)}, bf16[640,1280]{1,0:T(8,128)(2,1)S(1)}, u32[]{:S(2)}, u32[]{:S(2)}) collective-permute-start(bf16[640,1280]{1,0:T(8,128)(2,1)S(1)} %shard_map.58), channel_id=1, source_target_pairs={{0,72},{1,65},{2,74},{3,67},{4,76},{5,69},{6,78},{7,71},{64,0},{65... | collective-permute-start | bytes 4915208 | tf_op jit(solution)/shard_map/ppermute | solution.py:34
  50.8 7.5 %collective-permute-start.4 = (bf16[640,640]{1,0:T(8,128)(2,1)S(1)}, bf16[640,640]{1,0:T(8,128)(2,1)S(1)}, u32[]{:S(2)}, u32[]{:S(2)}) collective-permute-start(bf16[640,640]{1,0:T(8,128)(2,1)S(1)} %collective-permute-done.2.refs_4_), channel_id=1, source_target_pairs={{0,1},{1,0},{2,3},{3,2},{4,5},{5,4},{6,7},{7,6},{64,65},{65,64},{6... | collective-permute-start | bytes 2457608 | tf_op jit(solution)/shard_map/ppermute | solution.py:34
  54.4 14.8 %collective-permute-start.7 = (bf16[640,640]{1,0:T(8,128)(2,1)S(1)}, bf16[640,640]{1,0:T(8,128)(2,1)S(1)}, u32[]{:S(2)}, u32[]{:S(2)}) collective-permute-start(bf16[640,640]{1,0:T(8,128)(2,1)S(1)} %collective-permute-done.5.refs_7_.refs_5_), channel_id=1, source_target_pairs={{0,1},{1,0},{2,3},{3,2},{4,5},{5,4},{6,7},{7,6},{64,65},{65,64},{6... | collective-permute-start | bytes 2457608 | tf_op jit(solution)/shard_map/ppermute | solution.py:34
  54.4 1.7 %copy-start.3 = (bf16[384,2560]{1,0:T(8,128)(2,1)}, bf16[384,2560]{1,0:T(8,128)(2,1)S(1)}, u32[]{:S(2)}) copy-start(bf16[384,2560]{1,0:T(8,128)(2,1)S(1)} %collective-permute-done.x_oth) | copy-start | bytes 5898244
  54.4 14.8 %collective-permute-start.8 = (bf16[640,640]{1,0:T(8,128)(2,1)S(1)}, bf16[640,640]{1,0:T(8,128)(2,1)S(1)}, u32[]{:S(2)}, u32[]{:S(2)}) collective-permute-start(bf16[640,640]{1,0:T(8,128)(2,1)S(1)} %collective-permute-done.6.refs_8_.refs_6_), channel_id=1, source_target_pairs={{0,1},{1,0},{2,3},{3,2},{4,5},{5,4},{6,7},{7,6},{64,65},{65,64},{6... | collective-permute-start | bytes 2457608 | tf_op jit(solution)/shard_map/ppermute | solution.py:34
  63.8 18.7 %collective-permute-start.11 = (bf16[288,640]{1,0:T(8,128)(2,1)S(1)}, bf16[288,640]{1,0:T(8,128)(2,1)S(1)}, u32[]{:S(2)}, u32[]{:S(2)}) collective-permute-start(bf16[288,640]{1,0:T(8,128)(2,1)S(1)} %get-tuple-element.24.refs_0_.refs_2_), channel_id=1, source_target_pairs={{0,2},{1,3},{2,0},{3,1},{4,6},{5,7},{6,4},{7,5},{64,66},{65,67},{6... | collective-permute-start | bytes 1105928 | tf_op jit(solution)/shard_map/ppermute | solution.py:34
  73.2 5.6 %collective-permute-start.15 = (bf16[96,640]{1,0:T(8,128)(2,1)S(1)}, bf16[96,640]{1,0:T(8,128)(2,1)S(1)}, u32[]{:S(2)}, u32[]{:S(2)}) collective-permute-start(bf16[96,640]{1,0:T(8,128)(2,1)S(1)} %get-tuple-element.25), channel_id=1, source_target_pairs={{0,8},{1,9},{2,10},{3,11},{4,12},{5,13},{6,14},{7,15},{64,72},{65,... | collective-permute-start | bytes 368648 | tf_op jit(solution)/shard_map/ppermute | solution.py:34
  76.6 58.4 %collective-permute-start.23 = (bf16[640,1280]{1,0:T(8,128)(2,1)S(1)}, bf16[640,1280]{1,0:T(8,128)(2,1)S(1)}, u32[]{:S(2)}, u32[]{:S(2)}) collective-permute-start(bf16[640,1280]{1,0:T(8,128)(2,1)S(1)} %collective-permute-done.22.rem), channel_id=1, source_target_pairs={{0,1},{1,0},{2,3},{3,2},{4,5},{5,4},{6,7},{7,6},{64,65},{65,64},{6... | collective-permute-start | bytes 4915208 | tf_op jit(solution)/shard_map/ppermute | solution.py:34
  76.6 25.3 %collective-permute-start.19 = (bf16[384,640]{1,0:T(8,128)(2,1)S(1)}, bf16[384,640]{1,0:T(8,128)(2,1)S(1)}, u32[]{:S(2)}, u32[]{:S(2)}) collective-permute-start(bf16[384,640]{1,0:T(8,128)(2,1)S(1)} %get-tuple-element.28.refs_2_), channel_id=1, source_target_pairs={{0,2},{1,3},{2,0},{3,1},{4,6},{5,7},{6,4},{7,5},{64,66},{65,67},{6... | collective-permute-start | bytes 1474568 | tf_op jit(solution)/shard_map/ppermute | solution.py:34
  78.8 26.0 %collective-permute-start.16 = (bf16[384,640]{1,0:T(8,128)(2,1)S(1)}, bf16[384,640]{1,0:T(8,128)(2,1)S(1)}, u32[]{:S(2)}, u32[]{:S(2)}) collective-permute-start(bf16[384,640]{1,0:T(8,128)(2,1)S(1)} %shard_map.54.refs_7_), channel_id=1, source_target_pairs={{0,2},{1,3},{2,0},{3,1},{4,6},{5,7},{6,4},{7,5},{64,66},{65,67},{6... | collective-permute-start | bytes 1474568 | tf_op jit(solution)/shard_map/ppermute | solution.py:34
  78.9 12.7 %collective-permute-start.12 = (bf16[288,640]{1,0:T(8,128)(2,1)S(1)}, bf16[288,640]{1,0:T(8,128)(2,1)S(1)}, u32[]{:S(2)}, u32[]{:S(2)}) collective-permute-start(bf16[288,640]{1,0:T(8,128)(2,1)S(1)} %get-tuple-element.24.refs_0_.refs_2_), channel_id=1, source_target_pairs={{0,6},{1,7},{2,4},{3,5},{4,2},{5,3},{6,0},{7,1},{64,70},{65,71},{6... | collective-permute-start | bytes 1105928 | tf_op jit(solution)/shard_map/ppermute | solution.py:34
  82.5 16.7 %collective-permute-start.13 = (bf16[288,640]{1,0:T(8,128)(2,1)S(1)}, bf16[288,640]{1,0:T(8,128)(2,1)S(1)}, u32[]{:S(2)}, u32[]{:S(2)}) collective-permute-start(bf16[288,640]{1,0:T(8,128)(2,1)S(1)} %collective-permute-done.11.refs_1_.refs_3_), channel_id=1, source_target_pairs={{0,6},{1,7},{2,4},{3,5},{4,2},{5,3},{6,0},{7,1},{64,70},{65,71},{6... | collective-permute-start | bytes 1105928 | tf_op jit(solution)/shard_map/ppermute | solution.py:34
  91.7 22.8 %collective-permute-start.20 = (bf16[384,640]{1,0:T(8,128)(2,1)S(1)}, bf16[384,640]{1,0:T(8,128)(2,1)S(1)}, u32[]{:S(2)}, u32[]{:S(2)}) collective-permute-start(bf16[384,640]{1,0:T(8,128)(2,1)S(1)} %get-tuple-element.29.refs_4_), channel_id=1, source_target_pairs={{0,2},{1,3},{2,0},{3,1},{4,6},{5,7},{6,4},{7,5},{64,66},{65,67},{6... | collective-permute-start | bytes 1474568 | tf_op jit(solution)/shard_map/ppermute | solution.py:34
  99.2 18.6 %collective-permute-start.14 = (bf16[384,640]{1,0:T(8,128)(2,1)S(1)}, bf16[384,640]{1,0:T(8,128)(2,1)S(1)}, u32[]{:S(2)}, u32[]{:S(2)}) collective-permute-start(bf16[384,640]{1,0:T(8,128)(2,1)S(1)} %shard_map.51), channel_id=1, source_target_pairs={{0,8},{1,9},{2,10},{3,11},{4,12},{5,13},{6,14},{7,15},{64,72},{65,... | collective-permute-start | bytes 1474568 | tf_op jit(solution)/shard_map/ppermute | solution.py:34
  101.9 16.0 %collective-permute-start.17 = (bf16[384,640]{1,0:T(8,128)(2,1)S(1)}, bf16[384,640]{1,0:T(8,128)(2,1)S(1)}, u32[]{:S(2)}, u32[]{:S(2)}) collective-permute-start(bf16[384,640]{1,0:T(8,128)(2,1)S(1)} %shard_map.54.refs_7_), channel_id=1, source_target_pairs={{0,6},{1,7},{2,4},{3,5},{4,2},{5,3},{6,0},{7,1},{64,70},{65,71},{6... | collective-permute-start | bytes 1474568 | tf_op jit(solution)/shard_map/ppermute | solution.py:34
  104.9 21.5 %collective-permute-start.18 = (bf16[384,640]{1,0:T(8,128)(2,1)S(1)}, bf16[384,640]{1,0:T(8,128)(2,1)S(1)}, u32[]{:S(2)}, u32[]{:S(2)}) collective-permute-start(bf16[384,640]{1,0:T(8,128)(2,1)S(1)} %collective-permute-done.16.refs_8_), channel_id=1, source_target_pairs={{0,6},{1,7},{2,4},{3,5},{4,2},{5,3},{6,0},{7,1},{64,70},{65,71},{6... | collective-permute-start | bytes 1474568 | tf_op jit(solution)/shard_map/ppermute | solution.py:34
  126.3 6.3 %copy-start = (bf16[1280,1280]{1,0:T(8,128)(2,1)S(1)}, bf16[1280,1280]{1,0:T(8,128)(2,1)}, u32[]{:S(2)}) copy-start(bf16[1280,1280]{1,0:T(8,128)(2,1)} %w_loc.3) | copy-start | bytes 9830404
  131.1 3.8 %collective-permute-start.21 = (bf16[384,640]{1,0:T(8,128)(2,1)S(1)}, bf16[384,640]{1,0:T(8,128)(2,1)S(1)}, u32[]{:S(2)}, u32[]{:S(2)}) collective-permute-start(bf16[384,640]{1,0:T(8,128)(2,1)S(1)} %get-tuple-element.39), channel_id=1, source_target_pairs={{0,1},{1,0},{2,3},{3,2},{4,5},{5,4},{6,7},{7,6},{64,65},{65,64},{6... | collective-permute-start | bytes 1474568 | tf_op jit(solution)/shard_map/ppermute | solution.py:34
